TPU v7x, 32 devices: a whole 2x2x4 slice. The times are simulated.
32 devices in a mesh: group: 4 (over y, core), expert: 8 (over z, x).
Axes of the slice: x: 2, y: 2, z: 4, core: 2. Of those that a mesh axis runs over, the one named last changes fastest.
Arguments:
- tokens: bfloat16 [4096, 4096], P(('group', 'expert')), may hold values from -8 to 8
- router_weight: bfloat16 [4096, 128], replicated, may hold values from -4 to 4
- expert_dest: int32 [4096, 8], P(('group', 'expert')), may hold values from 0 to 127, all different within a row; in each aligned block of 128 rows (0 to 127, 128 to 255, ...) at most 9 rows name the same one
- group_capacity: int32 [4], replicated, may hold values from 4096 to 16383
- expert_capacity: int32 [128], replicated, may hold values from 128 to 511
- w_gate: bfloat16 [128, 4096, 768], P(('group', 'expert')), may hold values from -0.09375 to 0.09375
- w_up: bfloat16 [128, 4096, 768], P(('group', 'expert')), may hold values from -0.09375 to 0.09375
- w_down: bfloat16 [128, 768, 4096], P(('group', 'expert')), may hold values from -0.21875 to 0.21875
Outputs:
- mixed: bfloat16 [4096, 4096], P(('group', 'expert'))
- gating: float32 [4096, 8], P(('group', 'expert'))
Inputs may be any that keep to these rules, and one draw needn't show every extreme that they name: `expert_dest`: each token names 8 different experts; among the tokens of one device no expert is named more than 9 times, and that bound is reached.
All inputs are finite; a program needn't handle non-finite values.
Results may differ from a plain program's by a relative error of at most 0.0058.
Values may be sent and summed in bfloat16 or wider, within the bound.
No kernel may reach another device: no remote copies, remote signals or barrier semaphores. Data moves between devices by JAX's collectives and lax.ppermute only.
A program may use at most 256 MiB of HBM per device.

v0:
```python
import functools

import jax
import jax.numpy as jnp
from jax import lax
from jax.experimental import pallas as pl
from jax.experimental.pallas import tpu as pltpu
from jax.sharding import Mesh
from jax.sharding import PartitionSpec as P


ITER1 = 10
ITER2 = 10
SLOT_CAP = 9
MAIN = 8

ALL = ("group", "plane", "side")
PLANE = ("group", "side")
VMEM = pl.BlockSpec(memory_space=pltpu.VMEM)
SMEM = pl.BlockSpec(memory_space=pltpu.SMEM)
BIG = pltpu.CompilerParams(vmem_limit_bytes=60 << 20)


def round_up(value, step):
    return -(-value // step) * step


def piece_rows(exp_dev):
    return round_up(2 * exp_dev * SLOT_CAP, 8)


def row_slots(exp_dev, shape):
    row = lax.broadcasted_iota(jnp.int32, shape, 0)
    last = row - 2 * MAIN * exp_dev
    main = last < 0
    expert = jnp.where(main, lax.shift_right_logical(row, 4), lax.shift_right_logical(last, 1))
    half = jnp.where(main, lax.shift_right_logical(row, 3) & 1, last & 1)
    rank = jnp.where(main, row & 7, MAIN)
    slot = jnp.where(last >= 2 * exp_dev, -1, expert * SLOT_CAP + rank)
    return slot, half


def pack_kernel(exp_dev, dst_ref, slot_ref, tok_ref, *outs):
    rows, half_width = outs[0].shape
    topk, count = slot_ref.shape
    local, half = row_slots(exp_dev, (rows, count))
    low, high = [], []
    for k in range(len(outs)):
        want = jnp.where(local < 0, -1, local + dst_ref[k] * (exp_dev * SLOT_CAP))
        hit = jnp.zeros((rows, count), jnp.float32)
        for i in range(topk):
            hit = jnp.where(slot_ref[i : i + 1, :] == want, 1.0, hit)
        low.append(jnp.where(half == 0, hit, 0.0))
        high.append(jnp.where(half == 1, hit, 0.0))
    pick = jnp.concatenate(
        [jnp.concatenate(low, 0), jnp.concatenate(high, 0)], 1
    ).astype(jnp.bfloat16)
    step = min(512, half_width)
    for c in range(0, half_width, step):
        both = jnp.concatenate(
            [tok_ref[:, h * half_width + c : h * half_width + c + step] for h in range(2)], 0
        )
        got = jnp.dot(pick, both, preferred_element_type=jnp.float32)
        for k, out in enumerate(outs):
            out[:, c : c + step] = got[k * rows : (k + 1) * rows].astype(jnp.bfloat16)


def pack(exp_dev, dst, slot, tok):
    rows, width = piece_rows(exp_dev), tok.shape[1]
    n = dst.shape[0]
    return pl.pallas_call(
        functools.partial(pack_kernel, exp_dev),
        out_shape=[jax.ShapeDtypeStruct((rows, width // 2), jnp.bfloat16)] * n,
        in_specs=[SMEM, VMEM, VMEM],
        out_specs=[VMEM] * n,
        compiler_params=BIG,
        cost_estimate=pl.CostEstimate(
            flops=2 * n * rows * tok.shape[0] * width,
            bytes_accessed=2 * tok.size + n * rows * width,
            transcendentals=0,
        ),
        name="pack",
    )(dst, slot, tok)


def ffn_kernel(n, exp_dev, low, high, *refs):
    final = high == exp_dev
    refs = list(refs)

    def take(many):
        got = refs[:many]
        del refs[:many]
        return got

    mains, tails = take(n), take(n)
    weights = take(3)
    if low:
        (given_ref,) = take(1)
        take(n)
    outs = take(n)
    if not final:
        (rest_ref,) = take(1)
    x_ref, last_ref, res_ref, gate_ref, up_ref, down_ref, sems = refs
    buffers = (gate_ref, up_ref, down_ref)
    step_id = pl.program_id(0)
    half_width = mains[0].shape[1]
    step = min(1024, half_width)
    many = high - low

    def load(e, j):
        slot = lax.rem(e, 2)
        return pltpu.make_async_copy(weights[j].at[low + e], buffers[j].at[slot], sems.at[slot, j])

    @pl.when(step_id == 0)
    def _():
        for e in range(min(2, many)):
            for j in range(3):
                load(e, j).start()
        for c in range(0, half_width, step):
            tiles = [p[:8, c : c + step].astype(jnp.float32) for p in tails]
            last_ref[:, c : c + step] = jnp.concatenate(tiles, 0).astype(jnp.bfloat16)
        if low:
            res_ref[: low * n, :] = given_ref[...]

    @pl.when(step_id < many)
    def _():
        e = step_id
        for i in range(0, n, 2):
            for c in range(0, half_width, step):
                a = mains[i][:, c : c + step].astype(jnp.float32)
                b = mains[i + 1][:, c : c + step].astype(jnp.float32)
                for h in range(2):
                    both = jnp.concatenate([a[h * 8 : h * 8 + 8], b[h * 8 : h * 8 + 8]], 0)
                    x_ref[i * 8 : i * 8 + 16, h * half_width + c : h * half_width + c + step] = (
                        both.astype(jnp.bfloat16)
                    )
        row = lax.broadcasted_iota(jnp.int32, (n, 8 * n), 0)
        col = lax.broadcasted_iota(jnp.int32, (n, 8 * n), 1)
        for h in range(2):
            pick = jnp.where(col == row * 8 + (low + e) * 2 + h, 1.0, 0.0).astype(jnp.bfloat16)
            for c in range(0, half_width, step):
                x_ref[8 * n :, h * half_width + c : h * half_width + c + step] = jnp.dot(
                    pick, last_ref[:, c : c + step], preferred_element_type=jnp.float32
                ).astype(jnp.bfloat16)
        slot = lax.rem(e, 2)
        rest = pl.ds(pl.multiple_of((low + e) * n, n), n)
        load(e, 0).wait()
        gate = jnp.dot(x_ref[...], gate_ref[slot], preferred_element_type=jnp.float32)
        load(e, 1).wait()
        up = jnp.dot(x_ref[...], up_ref[slot], preferred_element_type=jnp.float32)
        hidden = (gate / (1.0 + jnp.exp(-gate)) * up).astype(jnp.bfloat16)
        load(e, 2).wait()
        for c in range(0, half_width, step):
            down = [
                jnp.dot(
                    hidden,
                    down_ref[slot, :, h * half_width + c : h * half_width + c + step],
                    preferred_element_type=jnp.float32,
                )
                for h in range(2)
            ]
            for i in range(n):
                both = jnp.concatenate([d[i * 8 : i * 8 + 8] for d in down], 0)
                outs[i][:, c : c + step] = both.astype(jnp.bfloat16)
            for h in range(2):
                res_ref[rest, h * half_width + c : h * half_width + c + step] = down[h][
                    8 * n :
                ].astype(jnp.bfloat16)

    @pl.when(step_id + 2 < many)
    def _():
        for j in range(3):
            load(step_id + 2, j).start()

    if not final:

        @pl.when(step_id == many - 1)
        def _():
            rest_ref[...] = res_ref[: high * n, :]

    else:

        @pl.when(step_id == many)
        def _():
            row = lax.broadcasted_iota(jnp.int32, (8 * n, exp_dev * n), 0)
            col = lax.broadcasted_iota(jnp.int32, (8 * n, exp_dev * n), 1)
            hit = col == lax.shift_right_logical(row & 7, 1) * n + lax.shift_right_logical(row, 3)
            for c in range(0, half_width, step):
                got = None
                for h in range(2):
                    pick = jnp.where(hit & ((row & 1) == h), 1.0, 0.0).astype(jnp.bfloat16)
                    term = jnp.dot(
                        pick,
                        res_ref[:, h * half_width + c : h * half_width + c + step],
                        preferred_element_type=jnp.float32,
                    )
                    got = term if got is None else got + term
                for i in range(n):
                    outs[i][:8, c : c + step] = got[i * 8 : i * 8 + 8].astype(jnp.bfloat16)


def ffn(pieces, w_gate, w_up, w_down, low, high, so_far=()):
    n = len(pieces)
    exp_dev, width, hidden = w_gate.shape
    rows, half_width = pieces[0].shape
    final = high == exp_dev
    tile = 2 * MAIN
    main = pl.BlockSpec((tile, half_width), lambda e: (jnp.minimum(low + e, exp_dev - 1), 0))
    tail = pl.BlockSpec((tile, half_width), lambda e: (exp_dev, 0), pipeline_mode=pl.Buffered(1))
    made = pl.BlockSpec((tile, half_width), lambda e: (low + e, 0))
    whole = pl.BlockSpec(memory_space=pl.ANY)
    total = SLOT_CAP * n
    in_specs = [main] * n + [tail] * n + [whole] * 3
    args = [*pieces, *pieces, w_gate, w_up, w_down]
    aliases = {}
    if low:
        before, given = so_far[:n], so_far[n]
        in_specs += [pl.BlockSpec((low * n, width), lambda e: (0, 0))] + [whole] * n
        aliases = {len(args) + 1 + i: i for i in range(n)}
        args += [given, *before]
    out_shape = [jax.ShapeDtypeStruct((rows, half_width), jnp.bfloat16)] * n
    out_specs = [made] * n
    if not final:
        out_shape.append(jax.ShapeDtypeStruct((high * n, width), jnp.bfloat16))
        out_specs.append(pl.BlockSpec((high * n, width), lambda e: (0, 0)))
    return pl.pallas_call(
        functools.partial(ffn_kernel, n, exp_dev, low, high),
        grid=(high - low + (1 if final else 0),),
        out_shape=out_shape,
        in_specs=in_specs,
        out_specs=out_specs,
        input_output_aliases=aliases,
        scratch_shapes=[
            pltpu.VMEM((total, width), jnp.bfloat16),
            pltpu.VMEM((8 * n, half_width), jnp.bfloat16),
            pltpu.VMEM((exp_dev * n, width), jnp.bfloat16),
            pltpu.VMEM((2, width, hidden), jnp.bfloat16),
            pltpu.VMEM((2, width, hidden), jnp.bfloat16),
            pltpu.VMEM((2, hidden, width), jnp.bfloat16),
            pltpu.SemaphoreType.DMA((2, 3)),
        ],
        compiler_params=pltpu.CompilerParams(
            dimension_semantics=("arbitrary",), vmem_limit_bytes=60 << 20
        ),
        cost_estimate=pl.CostEstimate(
            flops=6 * (high - low) * total * width * hidden,
            bytes_accessed=6 * (high - low) * width * hidden + 4 * n * rows * half_width,
            transcendentals=(high - low) * total * hidden,
        ),
        name="ffn",
    )(*args)


def combine_kernel(exp_dev, n, halves, joined, dst_ref, slot_ref, gate_ref, *refs):
    outs = refs[-1:] if joined else refs[-len(halves) :]
    pieces, others = refs[:n], refs[n : -len(outs)]
    rows, half_width = pieces[0].shape
    topk, count = slot_ref.shape
    local, half = row_slots(exp_dev, (rows, count))
    depth = round_up(n * rows, 128)
    fill = depth - n * rows
    weights = []
    for k in range(n):
        want = jnp.where(local < 0, -1, local + dst_ref[k] * (exp_dev * SLOT_CAP))
        weight = jnp.zeros((rows, count), jnp.float32)
        for i in range(topk):
            weight = jnp.where(slot_ref[i : i + 1, :] == want, gate_ref[i : i + 1, :], weight)
        weights.append(weight)
    coarse, rest = [], []
    for h in halves:
        parts = [jnp.where(half == h, weight, 0.0) for weight in weights]
        if fill:
            parts.append(jnp.zeros((fill, count), jnp.float32))
        turned = jnp.concatenate(parts, 0).T
        coarse.append(turned.astype(jnp.bfloat16))
        rest.append((turned - coarse[-1].astype(jnp.float32)).astype(jnp.bfloat16))
    weights = jnp.concatenate(coarse + rest, 0)
    step = min(512, half_width)
    for c in range(0, half_width, step):
        parts = [piece[:, c : c + step].astype(jnp.float32) for piece in pieces]
        if fill:
            parts.append(jnp.zeros((fill, step), jnp.float32))
        total = jnp.dot(
            weights,
            jnp.concatenate(parts, 0).astype(jnp.bfloat16),
            preferred_element_type=jnp.float32,
        )
        m = len(halves)
        for i, h in enumerate(halves):
            value = total[i * count : (i + 1) * count]
            value = value + total[(m + i) * count : (m + i + 1) * count]
            for other in others[i::m]:
                value = value + other[:, c : c + step].astype(jnp.float32)
            value = value.astype(jnp.bfloat16)
            if joined:
                outs[0][:, h * half_width + c : h * half_width + c + step] = value
            else:
                outs[i][:, c : c + step] = value


def combine(exp_dev, dst, slot, gate, pieces, others=(), halves=(0, 1), joined=False):
    n, m = len(pieces), len(halves)
    rows, half_width = pieces[0].shape
    count = slot.shape[1]
    wide = 2 * half_width if joined else half_width
    return pl.pallas_call(
        functools.partial(combine_kernel, exp_dev, n, halves, joined),
        out_shape=[jax.ShapeDtypeStruct((count, wide), jnp.bfloat16)] * (1 if joined else m),
        in_specs=[SMEM] + [VMEM] * (2 + n + len(others)),
        out_specs=[VMEM] * (1 if joined else m),
        compiler_params=BIG,
        cost_estimate=pl.CostEstimate(
            flops=4 * m * n * rows * count * half_width,
            bytes_accessed=2 * n * rows * half_width + 2 * (m + len(others)) * count * half_width,
            transcendentals=0,
        ),
        name="combine",
    )(dst, slot, gate, *pieces, *others)


def balance_kernel(n_group, size, mine_ref, own_ref, gt_ref, et_ref, *refs):
    blocks, (plan_ref, fac_ref) = refs[:-2], refs[-2:]
    sums = [[b[:, size + g, :] for g in range(n_group)] for b in blocks]
    targets = [gt_ref[g : g + 1, :] for g in range(n_group)]
    lanes = own_ref.shape[1]

    def inverse(parts, scale):
        return 1.0 / sum(part * s for part, s in zip(parts, scale))

    def first(carry):
        scale = carry[:n_group]
        rows = [inverse(s, scale) for s in sums]
        new = []
        for g in range(n_group):
            total = sum(s[g] * r for s, r in zip(sums, rows))
            total = jnp.sum(jnp.sum(total, 0, keepdims=True), 1, keepdims=True)
            new.append(targets[g] / jnp.broadcast_to(total, (1, lanes)))
        return tuple(new) + scale

    scales = tuple(jnp.ones((1, lanes), jnp.float32) for _ in range(2 * n_group))
    for _ in range(ITER1):
        scales = first(scales)
    now, before = scales[:n_group], scales[n_group:]
    own = [own_ref[g : g + 1, :] for g in range(n_group)]
    own_rows = inverse(own, before)
    for g in range(n_group):
        plan_ref[g : g + 1, :] = own_rows * own[g] * now[g]
    mine = mine_ref[0]
    plans = []
    for s in sums:
        rows = inverse(s, before)
        chosen = sum(jnp.where(mine == g, s[g] * now[g], 0.0) for g in range(n_group))
        plans.append(rows * chosen)

    fac_ref[...] = jnp.ones_like(fac_ref)

    @pl.loop(0, ITER2)
    def _(step):
        fac = fac_ref[size:, :]
        total = jnp.zeros((size, lanes), jnp.float32)
        for b, plan in zip(blocks, plans):
            scores = b[:, :size, :]
            row = plan / jnp.sum(scores * fac[None], 1)
            total = total + jnp.sum(scores * row[:, None, :], 0)
        total = jnp.broadcast_to(jnp.sum(total, 1, keepdims=True), (size, lanes))
        fac_ref[:size, :] = fac
        fac_ref[size:, :] = et_ref[...] / total


def gating_kernel(size, factor, group_ref, scores_ref, plan_ref, dest_ref, *refs):
    facs, out_ref = refs[:-1], refs[-1]
    topk, count = dest_ref.shape
    total = [jnp.zeros((1, count), jnp.float32) for _ in range(topk)]
    index = lax.broadcasted_iota(jnp.int32, (size, count), 0)
    for k, fac in enumerate(facs):
        group = group_ref[k]
        scores = scores_ref[pl.ds(pl.multiple_of(group * size, 8), size), :]
        row = plan_ref[pl.ds(group, 1), :] / jnp.sum(scores * fac[:size, :], 0, keepdims=True)
        balanced = row * scores * fac[size:, :]
        expert = index + group * size
        for i in range(topk):
            hit = jnp.where(dest_ref[i : i + 1, :] == expert, balanced, 0.0)
            total[i] = total[i] + jnp.sum(hit, 0, keepdims=True)
    for i in range(topk):
        out_ref[i : i + 1, :] = total[i] * factor


def per_device(
    tokens, router_weight, expert_dest, group_capacity, expert_capacity, w_gate, w_up, w_down
):
    count, _ = tokens.shape
    experts = router_weight.shape[1]
    topk = expert_dest.shape[1]
    n_group, n_plane, n_side = (lax.axis_size(a) for a in ALL)
    devices = n_group * n_plane * n_side
    exp_dev = w_gate.shape[0]
    size = experts // n_group
    n_peer = n_group * n_side
    group, plane, side = (lax.axis_index(a) for a in ALL)
    peer = group * n_side + side

    def cross(value, k, axis, n):
        return lax.ppermute(value, axis, [(i, i ^ k) for i in range(n)]) if k else value

    def shift(value, s):
        pairs = [(i, (i + s) % n_plane) for i in range(n_plane)]
        return lax.ppermute(value, "plane", pairs) if s % n_plane else value

    def after(value, *deps):
        return lax.optimization_barrier((value, *deps))[0]

    peers = [peer ^ k for k in range(n_peer)]
    dst = jnp.stack([((p // n_side) * n_plane + plane) * n_side + p % n_side for p in peers])
    dst = dst.astype(jnp.int32)

    half = n_plane // 2
    shifts = [0] + sorted(range(1, n_plane), key=lambda s: (min(s, n_plane - s), s))
    toks = {0: tokens}
    for s in shifts[1:]:
        step = 1 if s <= half else -1
        toks[s] = shift(toks[(s - step) % n_plane], step)

    named = expert_dest[:, :, None] == jnp.arange(experts, dtype=jnp.int32)[None, None, :]
    member = jnp.any(named, 1).astype(jnp.bfloat16)
    order = jnp.arange(count)
    earlier = (order[:, None] > order[None, :]).astype(jnp.bfloat16)
    before = jnp.dot(earlier, member, preferred_element_type=jnp.float32)
    rank = jnp.sum(jnp.where(named, before[:, None, :], 0.0), 2).astype(jnp.int32)
    dest_t = expert_dest.T
    slot_t = dest_t * SLOT_CAP + rank.T
    slots = {}
    for s in shifts:
        slots[s] = shift(slot_t, s)

    def send(pieces):
        out = []
        for k in range(n_peer):
            out.append(cross(pieces[k], k, PLANE, n_peer))
        return out

    def packed(s):
        return pack(exp_dev, dst, slots[s], toks[s])

    def feed(i):
        group_of = pairs[i]
        given = [p for s in group_of for p in came[s]]
        cut = exp_dev // 2 if i == 0 else 0
        so_far = ()
        if cut:
            so_far = ffn(given, w_gate, w_up, w_down, 0, cut)
        made = ffn(given, w_gate, w_up, w_down, cut, exp_dev, so_far)
        return {s: made[j * n_peer : (j + 1) * n_peer] for j, s in enumerate(group_of)}

    sent, came, made, back = {}, {}, {}, {}
    pairs = [shifts[i : i + 2] for i in range(0, n_plane, 2)]
    sent[0] = packed(0)
    came[0] = send(sent[0])

    logits = jnp.dot(
        tokens, after(router_weight, sent[0][0]), preferred_element_type=jnp.float32
    )
    scores = jnp.exp(logits).T
    pad = round_up(n_group, 8)
    sums = jnp.pad(jnp.sum(scores.reshape(n_group, size, count), 1), ((0, pad - n_group), (0, 0)))
    held = []
    for k in range(n_group):
        part = lax.dynamic_slice_in_dim(scores, (group ^ k) * size, size, 0)
        held.append(cross(jnp.concatenate([part, sums], 0), k, "group", n_group))

    last = None
    for s in pairs[0][1:]:
        sent[s] = packed(s)
        came[s] = send(sent[s])
        last = sent[s][0]
    if last is not None:
        held = [after(h, last) for h in held]
    held = jnp.stack(held)
    held = jnp.concatenate([held] + [cross(held, k, "side", n_side) for k in range(1, n_side)], 0)
    for s in shifts:
        if s not in sent and s in (pairs + [[]])[1]:
            sent[s] = packed(s)
            came[s] = send(sent[s])
    spread = []
    for s in shifts:
        spread.append(shift(held, s))
    made.update(feed(0))
    for s in shifts:
        if s not in sent:
            sent[s] = packed(s)
            came[s] = send(sent[s])

    gcap = group_capacity.astype(jnp.float32)
    gtarget = count * devices * gcap / jnp.sum(gcap)
    ecap = expert_capacity.astype(jnp.float32).reshape(n_group, size)
    etarget = (gtarget / jnp.sum(ecap, 1))[:, None] * ecap
    own_target = lax.dynamic_index_in_dim(etarget, group, 0, keepdims=False)
    plan, fac = pl.pallas_call(
        functools.partial(balance_kernel, n_group, size),
        out_shape=[
            jax.ShapeDtypeStruct((pad, count), jnp.float32),
            jax.ShapeDtypeStruct((2 * size, count), jnp.float32),
        ],
        in_specs=[SMEM] + [VMEM] * (3 + n_plane),
        out_specs=[VMEM] * 2,
        compiler_params=BIG,
        cost_estimate=pl.CostEstimate(
            flops=8 * ITER2 * experts * count * devices // n_group,
            bytes_accessed=4 * size * count * devices,
            transcendentals=0,
        ),
        name="balance",
    )(
        group.astype(jnp.int32)[None],
        after(sums, made[0][0]),
        jnp.broadcast_to(gtarget[:, None], (n_group, count)),
        jnp.broadcast_to(own_target[:, None], (size, count)),
        *spread,
    )
    facs = []
    for k in range(n_group):
        facs.append(cross(fac, k, "group", n_group))

    early = [s for s in pairs[0] if s]
    for s in early:
        back[s] = send([after(p, plan) for p in made[s]])
    for i in range(1, len(pairs)):
        made.update(feed(i))
    late = [s for group_of in pairs[1:] for s in group_of][::-1]
    for s in late:
        back[s] = send(made[s])

    gating_t = pl.pallas_call(
        functools.partial(gating_kernel, size, experts / topk),
        out_shape=jax.ShapeDtypeStruct((topk, count), jnp.float32),
        in_specs=[SMEM] + [VMEM] * (3 + n_group),
        out_specs=VMEM,
        compiler_params=BIG,
        name="gating",
    )(
        jnp.stack([group ^ k for k in range(n_group)]).astype(jnp.int32),
        scores,
        after(plan, made[late[-1]][0]) if late else plan,
        dest_t,
        *facs,
    )
    gates = {}
    for s in shifts:
        gates[s] = shift(gating_t, s)

    def combined(s, others, halves, joined=False):
        return combine(
            exp_dev, dst, slots[s], gates[s], back[s], others, halves=halves, joined=joined
        )

    back[0] = send(made[0])
    near = (n_plane - 1) // 2
    gone = []
    for chain, step in ((range(near, 0, -1), -1), (range(near + 1, n_plane), 1)):
        running = ()
        for s in chain:
            if running:
                value = [combined(s, running[h : h + 1], (h,))[0] for h in range(2)]
            else:
                value = combined(s, (), (0, 1))
            running = []
            for h in range(2):
                running.append(shift(value[h], step))
        gone += running
    mixed = combined(0, gone, (0, 1), joined=True)[0]
    return mixed, gating_t.T


def solution(mesh):
    n_group, n_lane = mesh.shape["group"], mesh.shape["expert"]
    n_side = 2 if n_lane % 2 == 0 else 1
    fine = Mesh(mesh.devices.reshape(n_group, n_lane // n_side, n_side), ALL)
    rows = P(ALL, None)
    stack = P(ALL, None, None)

    return jax.shard_map(
        per_device,
        mesh=fine,
        in_specs=(rows, P(), rows, P(), P(), stack, stack, stack),
        out_specs=(rows, rows),
        check_vma=False,
    )
```

profile of v0, /device:TPU:0, one launch (start us, length us, event | category | flops | bytes accessed | tf_op | source)
XLA Modules:
  0.0 397.8 jit_solution(17720714202513224587)
XLA Ops:
  0.6 3.1 collective-permute-start.8
  7.7 2.2 collective-permute-start.23
  11.7 3.5 pack.4
  19.2 10.9 %collective-permute-done.7.slot_ref = s32[8,128]{1,0:T(8,128)S(1)} collective-permute-done((s32[8,128]{1,0:T(8,128)S(1)}, s32[8,128]{1,0:T(8,128)S(1)}, u32[]{:S(2)}, u32[]{:S(2)}) %collective-permute-start.7) | collective-permute-done | bytes 4128 | tf_op jit(solution)/shard_map/ppermute | solution.py:407
  32.0 3.4 pack.5
  37.6 2.7 collective-permute-done.18
  40.9 11.0 %collective-permute-done.32.slot_ref = s32[8,128]{1,0:T(8,128)S(1)} collective-permute-done((s32[8,128]{1,0:T(8,128)S(1)}, s32[8,128]{1,0:T(8,128)S(1)}, u32[]{:S(2)}, u32[]{:S(2)}) %collective-permute-start.32) | collective-permute-done | bytes 4128 | tf_op jit(solution)/shard_map/ppermute | solution.py:407
  56.8 17.8 %collective-permute-done.3.refs_4_.refs_20_ = bf16[72,2048]{1,0:T(8,128)(2,1)S(1)} collective-permute-done((bf16[72,2048]{1,0:T(8,128)(2,1)}, bf16[72,2048]{1,0:T(8,128)(2,1)S(1)}, u32[]{:S(2)}, u32[]{:S(2)}) %collective-permute-start.3) | collective-permute-done | bytes 294944 | tf_op jit(solution)/shard_map/ppermute | solution.py:403
  76.8 3.2 collective-permute-done.19
  80.1 12.5 %collective-permute-start.21 = (f32[8,40,128]{2,1,0:T(8,128)S(1)}, f32[8,40,128]{2,1,0:T(8,128)S(1)}, u32[]{:S(2)}, u32[]{:S(2)}) collective-permute-start(f32[8,40,128]{2,1,0:T(8,128)S(1)} %constant_dynamic-update-slice_fusion.refs_0_), channel_id=1, source_target_pairs={{0,6},{2,0},{4,2},{6,4},{1,7},{3,1},{5,3},{7,5},{8,14},{10,8},{12,... | collective-permute-start | bytes 491528 | tf_op jit(solution)/shard_map/ppermute | solution.py:407
  95.3 2.3 collective-permute-done.20.refs_1_
  99.6 2.2 collective-permute-start.13
  105.7 3.4 pack.6
  109.1 9.7 %collective-permute-done.12.refs_12_.refs_28_ = bf16[72,2048]{1,0:T(8,128)(2,1)S(1)} collective-permute-done((bf16[72,2048]{1,0:T(8,128)(2,1)}, bf16[72,2048]{1,0:T(8,128)(2,1)S(1)}, u32[]{:S(2)}, u32[]{:S(2)}) %collective-permute-start.12) | collective-permute-done | bytes 294944 | tf_op jit(solution)/shard_map/ppermute | solution.py:403
  118.8 2.5 collective-permute-start.25
  123.1 3.4 collective-permute-start.27
  126.5 4.0 collective-permute-start.22
  130.5 16.2 %ffn.3 = (bf16[72,2048]{1,0:T(8,128)(2,1)}, bf16[72,2048]{1,0:T(8,128)(2,1)}, bf16[72,2048]{1,0:T(8,128)(2,1)}, bf16[72,2048]{1,0:T(8,128)(2,1)}, bf16[72,2048]{...) custom-call(bf16[72,2048]{1,0:T(8,128)(2,1)} %get-tuple-element.104., ...), custom_call_target="tpu_custom_call" | custom-call | flops 5435817984 | bytes 47185920 | tf_op jit(solution)/shard_map/ffn/pallas_call | solution.py:226
  148.6 3.0 collective-permute-start.31
  151.6 16.5 %ffn.4 = (bf16[72,2048]{1,0:T(8,128)(2,1)}, bf16[72,2048]{1,0:T(8,128)(2,1)}, bf16[72,2048]{1,0:T(8,128)(2,1)}, bf16[72,2048]{1,0:T(8,128)(2,1)}, bf16[72,2048]{...) custom-call(bf16[72,2048]{1,0:T(8,128)(2,1)} %get-tuple-element.104., ...), custom_call_target="tpu_custom_call", output_to_operand_aliasing={{0}: (36, {}), {1}: (37, {}), {2}: (38, {}), {3}: (39, {}),... | custom-call | flops 5435817984 | bytes 47185920 | tf_op jit(solution)/shard_map/ffn/pallas_call | solution.py:226
  169.4 4.9 %balance.1 = (f32[8,128]{1,0:T(8,128)}, f32[64,128]{1,0:T(8,128)}) custom-call(s32[1]{0:T(128)} %bitcast.10.mine_ref, f32[8,128]{1,0:T(8,128)} %copy-done.43, f32[4,128]{1,0:T(4,128)} %broadcast_in_dim.20.gt_ref, f32[32,128]{1,0:T(8,128)} %broadcast_in_dim.22.et_ref, f32[8,40,128]{2,1,0:T(8,128)} %copy-done.40, f32[8,40,128]{2,1,0:T(8,128)} %copy-done.41, ...), custom_call_target="tpu_custom_call" | custom-call | flops 10485760 | bytes 524288 | tf_op jit(solution)/shard_map/balance/pallas_call | solution.py:497
  176.3 3.4 pack.7
  179.8 2.0 collective-permute-start.52
  182.4 7.4 %collective-permute-done.44.refs_1_ = bf16[72,2048]{1,0:T(8,128)(2,1)S(1)} collective-permute-done((bf16[72,2048]{1,0:T(8,128)(2,1)}, bf16[72,2048]{1,0:T(8,128)(2,1)S(1)}, u32[]{:S(2)}, u32[]{:S(2)}) %collective-permute-start.44) | collective-permute-done | bytes 294944 | tf_op jit(solution)/shard_map/ppermute | solution.py:403
  189.9 6.3 %collective-permute-done.52.refs_1_ = bf16[72,2048]{1,0:T(8,128)(2,1)S(1)} collective-permute-done((bf16[72,2048]{1,0:T(8,128)(2,1)}, bf16[72,2048]{1,0:T(8,128)(2,1)S(1)}, u32[]{:S(2)}, u32[]{:S(2)}) %collective-permute-start.52) | collective-permute-done | bytes 294944 | tf_op jit(solution)/shard_map/ppermute | solution.py:403
  199.1 3.4 collective-permute-done.34.refs_9_.refs_25_
  203.7 3.9 collective-permute-done.36.refs_11_.refs_27_
  209.7 6.0 %collective-permute-done.38.refs_13_.refs_29_ = bf16[72,2048]{1,0:T(8,128)(2,1)S(1)} collective-permute-done((bf16[72,2048]{1,0:T(8,128)(2,1)}, bf16[72,2048]{1,0:T(8,128)(2,1)S(1)}, u32[]{:S(2)}, u32[]{:S(2)}) %collective-permute-start.38) | collective-permute-done | bytes 294944 | tf_op jit(solution)/shard_map/ppermute | solution.py:403
  216.1 8.6 %collective-permute-done.39.refs_14_.refs_30_ = bf16[72,2048]{1,0:T(8,128)(2,1)} collective-permute-done((bf16[72,2048]{1,0:T(8,128)(2,1)}, bf16[72,2048]{1,0:T(8,128)(2,1)}, u32[]{:S(2)}, u32[]{:S(2)}) %collective-permute-start.39) | collective-permute-done | bytes 294944 | tf_op jit(solution)/shard_map/ppermute | solution.py:403
  226.0 31.7 %ffn.5 = (bf16[72,2048]{1,0:T(8,128)(2,1)}, bf16[72,2048]{1,0:T(8,128)(2,1)}, bf16[72,2048]{1,0:T(8,128)(2,1)}, bf16[72,2048]{1,0:T(8,128)(2,1)}, bf16[72,2048]{...) custom-call(bf16[72,2048]{1,0:T(8,128)(2,1)} %get-tuple-element.145., ...), custom_call_target="tpu_custom_call" | custom-call | flops 10871635968 | bytes 84934656 | tf_op jit(solution)/shard_map/ffn/pallas_call | solution.py:226
  257.7 2.1 collective-permute-start.70
  264.1 3.6 collective-permute-done.51.gate_ref
  269.2 3.1 collective-permute-start.76
  275.1 15.2 %collective-permute-done.73.refs_4_ = bf16[72,2048]{1,0:T(8,128)(2,1)S(1)} collective-permute-done((bf16[72,2048]{1,0:T(8,128)(2,1)}, bf16[72,2048]{1,0:T(8,128)(2,1)S(1)}, u32[]{:S(2)}, u32[]{:S(2)}) %collective-permute-start.73) | collective-permute-done | bytes 294944 | tf_op jit(solution)/shard_map/ppermute | solution.py:403
  290.5 3.2 collective-permute-done.75.refs_6_
  297.3 4.5 %combine.6 = (bf16[128,2048]{1,0:T(8,128)(2,1)}, bf16[128,2048]{1,0:T(8,128)(2,1)}) custom-call(s32[8]{0:T(128)} %stack.65.dst_ref, s32[8,128]{1,0:T(8,128)} %copy-done.64, f32[8,128]{1,0:T(8,128)} %copy-done.66, bf16[72,2048]{1,0:T(8,128)(2,1)} %get-tuple-element.196.refs_0_, bf16[72,2048]{1,0:T(8,128)(2,1)} %copy-done.56, bf16[72,2048]{1,0:T(8,128)(2,1)} %copy-done.57, ...), custom_call_target="tpu_custom_call" | custom-call | flops 1207959552 | bytes 3407872 | tf_op jit(solution)/shard_map/combine/pallas_call | solution.py:306
  307.7 7.4 %collective-permute-done.66.refs_5_ = bf16[72,2048]{1,0:T(8,128)(2,1)S(1)} collective-permute-done((bf16[72,2048]{1,0:T(8,128)(2,1)}, bf16[72,2048]{1,0:T(8,128)(2,1)S(1)}, u32[]{:S(2)}, u32[]{:S(2)}) %collective-permute-start.66) | collective-permute-done | bytes 294944 | tf_op jit(solution)/shard_map/ppermute | solution.py:403
  315.1 10.7 %collective-permute-done.67.refs_6_ = bf16[72,2048]{1,0:T(8,128)(2,1)S(1)} collective-permute-done((bf16[72,2048]{1,0:T(8,128)(2,1)}, bf16[72,2048]{1,0:T(8,128)(2,1)S(1)}, u32[]{:S(2)}, u32[]{:S(2)}) %collective-permute-start.67) | collective-permute-done | bytes 294944 | tf_op jit(solution)/shard_map/ppermute | solution.py:403
  327.0 2.1 collective-permute-start.48
  329.1 4.4 %combine.5 = (bf16[128,2048]{1,0:T(8,128)(2,1)}, bf16[128,2048]{1,0:T(8,128)(2,1)}) custom-call(s32[8]{0:T(128)} %stack.65.dst_ref, s32[8,128]{1,0:T(8,128)} %copy-done.63, f32[8,128]{1,0:T(8,128)} %copy-done.65, bf16[72,2048]{1,0:T(8,128)(2,1)} %get-tuple-element.172.refs_0_, bf16[72,2048]{1,0:T(8,128)(2,1)} %copy-done.54, bf16[72,2048]{1,0:T(8,128)(2,1)} %copy-done.55, ...), custom_call_target="tpu_custom_call" | custom-call | flops 1207959552 | bytes 3407872 | tf_op jit(solution)/shard_map/combine/pallas_call | solution.py:306
  334.0 3.6 combine.7
  337.6 3.7 combine.8
  341.3 3.2 collective-permute-start.59
  349.9 8.8 %collective-permute-done.50.refs_7_ = bf16[72,2048]{1,0:T(8,128)(2,1)S(1)} collective-permute-done((bf16[72,2048]{1,0:T(8,128)(2,1)}, bf16[72,2048]{1,0:T(8,128)(2,1)S(1)}, u32[]{:S(2)}, u32[]{:S(2)}) %collective-permute-start.50) | collective-permute-done | bytes 294944 | tf_op jit(solution)/shard_map/ppermute | solution.py:403
  358.7 9.7 %collective-permute-done.60.refs_9_ = bf16[128,2048]{1,0:T(8,128)(2,1)S(1)} collective-permute-done((bf16[128,2048]{1,0:T(8,128)(2,1)}, bf16[128,2048]{1,0:T(8,128)(2,1)S(1)}, u32[]{:S(2)}, u32[]{:S(2)}) %collective-permute-start.60) | collective-permute-done | bytes 524320 | tf_op jit(solution)/shard_map/ppermute | solution.py:407
  368.4 12.4 %collective-permute-done.78.refs_10_ = bf16[128,2048]{1,0:T(8,128)(2,1)S(1)} collective-permute-done((bf16[128,2048]{1,0:T(8,128)(2,1)}, bf16[128,2048]{1,0:T(8,128)(2,1)S(1)}, u32[]{:S(2)}, u32[]{:S(2)}) %collective-permute-start.78) | collective-permute-done | bytes 524320 | tf_op jit(solution)/shard_map/ppermute | solution.py:407
  380.8 11.0 %collective-permute-done.80.refs_11_ = bf16[128,2048]{1,0:T(8,128)(2,1)S(1)} collective-permute-done((bf16[128,2048]{1,0:T(8,128)(2,1)}, bf16[128,2048]{1,0:T(8,128)(2,1)S(1)}, u32[]{:S(2)}, u32[]{:S(2)}) %collective-permute-start.80) | collective-permute-done | bytes 524320 | tf_op jit(solution)/shard_map/ppermute | solution.py:407
  392.6 5.2 %combine.9 = bf16[128,4096]{1,0:T(8,128)(2,1)} custom-call(s32[8]{0:T(128)} %stack.65.dst_ref, s32[8,128]{1,0:T(8,128)} %copy-done.50, f32[8,128]{1,0:T(8,128)} %gating.1.gate_ref, bf16[72,2048]{1,0:T(8,128)(2,1)} %get-tuple-element.138.refs_0_, bf16[72,2048]{1,0:T(8,128)(2,1)} %copy-done.38, bf16[72,2048]{1,0:T(8,128)(2,1)} %collective-permute-done.45.refs_2_, ...), custom_call_target="tpu_custom_call" | custom-call | flops 1207959552 | bytes 5505024 | tf_op jit(solution)/shard_map/combine/pallas_call | solution.py:306
  (289 shorter events, 71.4 us)
Async XLA Ops:
  0.6 29.5 %collective-permute-start.8 = (bf16[128,4096]{1,0:T(8,128)(2,1)}, bf16[128,4096]{1,0:T(8,128)(2,1)S(1)}, u32[]{:S(2)}, u32[]{:S(2)}) collective-permute-start(bf16[128,4096]{1,0:T(8,128)(2,1)} %tok_ref.1), channel_id=1, source_target_pairs={{0,2},{2,4},{4,6},{6,0},{1,3},{3,5},{5,7},{7,1},{8,10},{10,12},{12... | collective-permute-start | bytes 3145736 | tf_op jit(solution)/shard_map/ppermute | solution.py:407
  6.1 24.1 %collective-permute-start.7 = (s32[8,128]{1,0:T(8,128)S(1)}, s32[8,128]{1,0:T(8,128)S(1)}, u32[]{:S(2)}, u32[]{:S(2)}) collective-permute-start(s32[8,128]{1,0:T(8,128)S(1)} %bitcast_add_fusion.slot_ref), channel_id=1, source_target_pairs={{0,2},{2,4},{4,6},{6,0},{1,3},{3,5},{5,7},{7,1},{8,10},{10,12},{12... | collective-permute-start | bytes 12296 | tf_op jit(solution)/shard_map/ppermute | solution.py:407
  7.7 32.9 %collective-permute-start.23 = (s32[8,128]{1,0:T(8,128)S(1)}, s32[8,128]{1,0:T(8,128)S(1)}, u32[]{:S(2)}, u32[]{:S(2)}) collective-permute-start(s32[8,128]{1,0:T(8,128)S(1)} %bitcast_add_fusion.slot_ref), channel_id=1, source_target_pairs={{0,6},{2,0},{4,2},{6,4},{1,7},{3,1},{5,3},{7,5},{8,14},{10,8},{12,... | collective-permute-start | bytes 12296 | tf_op jit(solution)/shard_map/ppermute | solution.py:407
  9.9 84.6 %collective-permute-start.24 = (bf16[128,4096]{1,0:T(8,128)(2,1)}, bf16[128,4096]{1,0:T(8,128)(2,1)}, u32[]{:S(2)}, u32[]{:S(2)}) collective-permute-start(bf16[128,4096]{1,0:T(8,128)(2,1)} %tok_ref.1), channel_id=1, source_target_pairs={{0,6},{2,0},{4,2},{6,4},{1,7},{3,1},{5,3},{7,5},{8,14},{10,8},{12,... | collective-permute-start | bytes 3145736 | tf_op jit(solution)/shard_map/ppermute | solution.py:407
  10.2 41.7 %collective-permute-start.32 = (s32[8,128]{1,0:T(8,128)S(1)}, s32[8,128]{1,0:T(8,128)S(1)}, u32[]{:S(2)}, u32[]{:S(2)}) collective-permute-start(s32[8,128]{1,0:T(8,128)S(1)} %bitcast_add_fusion.slot_ref), channel_id=1, source_target_pairs={{0,4},{2,6},{4,0},{6,2},{1,5},{3,7},{5,1},{7,3},{8,12},{10,14},{12... | collective-permute-start | bytes 12296 | tf_op jit(solution)/shard_map/ppermute | solution.py:407
  51.9 22.7 %collective-permute-start.3 = (bf16[72,2048]{1,0:T(8,128)(2,1)}, bf16[72,2048]{1,0:T(8,128)(2,1)S(1)}, u32[]{:S(2)}, u32[]{:S(2)}) collective-permute-start(bf16[72,2048]{1,0:T(8,128)(2,1)} %get-tuple-element.109), channel_id=1, source_target_pairs={{0,16},{1,17},{8,24},{9,25},{16,0},{17,1},{24,8},{25,9},{2,18},{3,... | collective-permute-start | bytes 884744 | tf_op jit(solution)/shard_map/ppermute | solution.py:403
  53.5 22.7 %collective-permute-start.4 = (bf16[72,2048]{1,0:T(8,128)(2,1)}, bf16[72,2048]{1,0:T(8,128)(2,1)S(1)}, u32[]{:S(2)}, u32[]{:S(2)}) collective-permute-start(bf16[72,2048]{1,0:T(8,128)(2,1)} %get-tuple-element.110), channel_id=1, source_target_pairs={{0,17},{1,16},{8,25},{9,24},{16,1},{17,0},{24,9},{25,8},{2,19},{3,... | collective-permute-start | bytes 884744 | tf_op jit(solution)/shard_map/ppermute | solution.py:403
  55.0 25.0 %collective-permute-start.5 = (bf16[72,2048]{1,0:T(8,128)(2,1)}, bf16[72,2048]{1,0:T(8,128)(2,1)S(1)}, u32[]{:S(2)}, u32[]{:S(2)}) collective-permute-start(bf16[72,2048]{1,0:T(8,128)(2,1)} %get-tuple-element.111), channel_id=1, source_target_pairs={{0,24},{1,25},{8,16},{9,17},{16,8},{17,9},{24,0},{25,1},{2,26},{3,... | collective-permute-start | bytes 884744 | tf_op jit(solution)/shard_map/ppermute | solution.py:403
  55.4 24.7 %collective-permute-start.6 = (bf16[72,2048]{1,0:T(8,128)(2,1)}, bf16[72,2048]{1,0:T(8,128)(2,1)S(1)}, u32[]{:S(2)}, u32[]{:S(2)}) collective-permute-start(bf16[72,2048]{1,0:T(8,128)(2,1)} %get-tuple-element.112), channel_id=1, source_target_pairs={{0,25},{1,24},{8,17},{9,16},{16,9},{17,8},{24,1},{25,0},{2,27},{3,... | collective-permute-start | bytes 884744 | tf_op jit(solution)/shard_map/ppermute | solution.py:403
  76.2 25.6 %collective-permute-start.9 = (bf16[72,2048]{1,0:T(8,128)(2,1)}, bf16[72,2048]{1,0:T(8,128)(2,1)S(1)}, u32[]{:S(2)}, u32[]{:S(2)}) collective-permute-start(bf16[72,2048]{1,0:T(8,128)(2,1)} %get-tuple-element.114), channel_id=1, source_target_pairs={{0,1},{1,0},{8,9},{9,8},{16,17},{17,16},{24,25},{25,24},{2,3},{3,2... | collective-permute-start | bytes 884744 | tf_op jit(solution)/shard_map/ppermute | solution.py:403
  80.0 21.9 %collective-permute-start.10 = (bf16[72,2048]{1,0:T(8,128)(2,1)}, bf16[72,2048]{1,0:T(8,128)(2,1)S(1)}, u32[]{:S(2)}, u32[]{:S(2)}) collective-permute-start(bf16[72,2048]{1,0:T(8,128)(2,1)} %get-tuple-element.115), channel_id=1, source_target_pairs={{0,8},{1,9},{8,0},{9,1},{16,24},{17,25},{24,16},{25,17},{2,10},{3,... | collective-permute-start | bytes 884744 | tf_op jit(solution)/shard_map/ppermute | solution.py:403
  80.1 19.4 %collective-permute-start.21 = (f32[8,40,128]{2,1,0:T(8,128)S(1)}, f32[8,40,128]{2,1,0:T(8,128)S(1)}, u32[]{:S(2)}, u32[]{:S(2)}) collective-permute-start(f32[8,40,128]{2,1,0:T(8,128)S(1)} %constant_dynamic-update-slice_fusion.refs_0_), channel_id=1, source_target_pairs={{0,6},{2,0},{4,2},{6,4},{1,7},{3,1},{5,3},{7,5},{8,14},{10,8},{12,... | collective-permute-start | bytes 491528 | tf_op jit(solution)/shard_map/ppermute | solution.py:407
  97.7 21.1 %collective-permute-start.12 = (bf16[72,2048]{1,0:T(8,128)(2,1)}, bf16[72,2048]{1,0:T(8,128)(2,1)S(1)}, u32[]{:S(2)}, u32[]{:S(2)}) collective-permute-start(bf16[72,2048]{1,0:T(8,128)(2,1)} %get-tuple-element.117), channel_id=1, source_target_pairs={{0,16},{1,17},{8,24},{9,25},{16,0},{17,1},{24,8},{25,9},{2,18},{3,... | collective-permute-start | bytes 884744 | tf_op jit(solution)/shard_map/ppermute | solution.py:403
  99.6 21.7 %collective-permute-start.13 = (bf16[72,2048]{1,0:T(8,128)(2,1)}, bf16[72,2048]{1,0:T(8,128)(2,1)S(1)}, u32[]{:S(2)}, u32[]{:S(2)}) collective-permute-start(bf16[72,2048]{1,0:T(8,128)(2,1)} %get-tuple-element.118), channel_id=1, source_target_pairs={{0,17},{1,16},{8,25},{9,24},{16,1},{17,0},{24,9},{25,8},{2,19},{3,... | collective-permute-start | bytes 884744 | tf_op jit(solution)/shard_map/ppermute | solution.py:403
  101.8 21.3 %collective-permute-start.14 = (bf16[72,2048]{1,0:T(8,128)(2,1)}, bf16[72,2048]{1,0:T(8,128)(2,1)S(1)}, u32[]{:S(2)}, u32[]{:S(2)}) collective-permute-start(bf16[72,2048]{1,0:T(8,128)(2,1)} %get-tuple-element.119), channel_id=1, source_target_pairs={{0,24},{1,25},{8,16},{9,17},{16,8},{17,9},{24,0},{25,1},{2,26},{3,... | collective-permute-start | bytes 884744 | tf_op jit(solution)/shard_map/ppermute | solution.py:403
  101.9 24.6 %collective-permute-start.15 = (bf16[72,2048]{1,0:T(8,128)(2,1)}, bf16[72,2048]{1,0:T(8,128)(2,1)S(1)}, u32[]{:S(2)}, u32[]{:S(2)}) collective-permute-start(bf16[72,2048]{1,0:T(8,128)(2,1)} %get-tuple-element.120), channel_id=1, source_target_pairs={{0,25},{1,24},{8,17},{9,16},{16,9},{17,8},{24,1},{25,0},{2,27},{3,... | collective-permute-start | bytes 884744 | tf_op jit(solution)/shard_map/ppermute | solution.py:403
  104.4 71.1 %collective-permute-start.33 = (bf16[128,4096]{1,0:T(8,128)(2,1)}, bf16[128,4096]{1,0:T(8,128)(2,1)}, u32[]{:S(2)}, u32[]{:S(2)}) collective-permute-start(bf16[128,4096]{1,0:T(8,128)(2,1)} %copy-done.53), channel_id=1, source_target_pairs={{0,2},{2,4},{4,6},{6,0},{1,3},{3,5},{5,7},{7,1},{8,10},{10,12},{12... | collective-permute-start | bytes 3145736 | tf_op jit(solution)/shard_map/ppermute | solution.py:407
  118.8 29.1 %collective-permute-start.25 = (bf16[72,2048]{1,0:T(8,128)(2,1)}, bf16[72,2048]{1,0:T(8,128)(2,1)}, u32[]{:S(2)}, u32[]{:S(2)}) collective-permute-start(bf16[72,2048]{1,0:T(8,128)(2,1)} %get-tuple-element.146), channel_id=1, source_target_pairs={{0,1},{1,0},{8,9},{9,8},{16,17},{17,16},{24,25},{25,24},{2,3},{3,2... | collective-permute-start | bytes 884744 | tf_op jit(solution)/shard_map/ppermute | solution.py:403
  121.3 26.6 %collective-permute-start.26 = (bf16[72,2048]{1,0:T(8,128)(2,1)}, bf16[72,2048]{1,0:T(8,128)(2,1)}, u32[]{:S(2)}, u32[]{:S(2)}) collective-permute-start(bf16[72,2048]{1,0:T(8,128)(2,1)} %get-tuple-element.147), channel_id=1, source_target_pairs={{0,8},{1,9},{8,0},{9,1},{16,24},{17,25},{24,16},{25,17},{2,10},{3,... | collective-permute-start | bytes 884744 | tf_op jit(solution)/shard_map/ppermute | solution.py:403
  123.1 25.5 %collective-permute-start.27 = (bf16[72,2048]{1,0:T(8,128)(2,1)}, bf16[72,2048]{1,0:T(8,128)(2,1)}, u32[]{:S(2)}, u32[]{:S(2)}) collective-permute-start(bf16[72,2048]{1,0:T(8,128)(2,1)} %get-tuple-element.148), channel_id=1, source_target_pairs={{0,9},{1,8},{8,1},{9,0},{16,25},{17,24},{24,17},{25,16},{2,11},{3,... | collective-permute-start | bytes 884744 | tf_op jit(solution)/shard_map/ppermute | solution.py:403
  126.5 20.3 %collective-permute-start.22 = (f32[8,40,128]{2,1,0:T(8,128)}, f32[8,40,128]{2,1,0:T(8,128)}, u32[]{:S(2)}, u32[]{:S(2)}) collective-permute-start(f32[8,40,128]{2,1,0:T(8,128)} %copy-done.40), channel_id=1, source_target_pairs={{0,4},{2,6},{4,0},{6,2},{1,5},{3,7},{5,1},{7,3},{8,12},{10,14},{12... | collective-permute-start | bytes 491528 | tf_op jit(solution)/shard_map/ppermute | solution.py:407
  146.8 27.5 %collective-permute-start.28 = (bf16[72,2048]{1,0:T(8,128)(2,1)}, bf16[72,2048]{1,0:T(8,128)(2,1)S(1)}, u32[]{:S(2)}, u32[]{:S(2)}) collective-permute-start(bf16[72,2048]{1,0:T(8,128)(2,1)} %get-tuple-element.149), channel_id=1, source_target_pairs={{0,16},{1,17},{8,24},{9,25},{16,0},{17,1},{24,8},{25,9},{2,18},{3,... | collective-permute-start | bytes 884744 | tf_op jit(solution)/shard_map/ppermute | solution.py:403
  147.9 26.5 %collective-permute-start.29 = (bf16[72,2048]{1,0:T(8,128)(2,1)}, bf16[72,2048]{1,0:T(8,128)(2,1)S(1)}, u32[]{:S(2)}, u32[]{:S(2)}) collective-permute-start(bf16[72,2048]{1,0:T(8,128)(2,1)} %get-tuple-element.150), channel_id=1, source_target_pairs={{0,17},{1,16},{8,25},{9,24},{16,1},{17,0},{24,9},{25,8},{2,19},{3,... | collective-permute-start | bytes 884744 | tf_op jit(solution)/shard_map/ppermute | solution.py:403
  147.9 31.8 %collective-permute-start.30 = (bf16[72,2048]{1,0:T(8,128)(2,1)}, bf16[72,2048]{1,0:T(8,128)(2,1)S(1)}, u32[]{:S(2)}, u32[]{:S(2)}) collective-permute-start(bf16[72,2048]{1,0:T(8,128)(2,1)} %get-tuple-element.151), channel_id=1, source_target_pairs={{0,24},{1,25},{8,16},{9,17},{16,8},{17,9},{24,0},{25,1},{2,26},{3,... | collective-permute-start | bytes 884744 | tf_op jit(solution)/shard_map/ppermute | solution.py:403
  148.6 31.2 %collective-permute-start.31 = (bf16[72,2048]{1,0:T(8,128)(2,1)}, bf16[72,2048]{1,0:T(8,128)(2,1)S(1)}, u32[]{:S(2)}, u32[]{:S(2)}) collective-permute-start(bf16[72,2048]{1,0:T(8,128)(2,1)} %get-tuple-element.152), channel_id=1, source_target_pairs={{0,25},{1,24},{8,17},{9,16},{16,9},{17,8},{24,1},{25,0},{2,27},{3,... | collective-permute-start | bytes 884744 | tf_op jit(solution)/shard_map/ppermute | solution.py:403
  181.8 20.7 %collective-permute-start.34 = (bf16[72,2048]{1,0:T(8,128)(2,1)}, bf16[72,2048]{1,0:T(8,128)(2,1)S(1)}, u32[]{:S(2)}, u32[]{:S(2)}) collective-permute-start(bf16[72,2048]{1,0:T(8,128)(2,1)} %get-tuple-element.154), channel_id=1, source_target_pairs={{0,1},{1,0},{8,9},{9,8},{16,17},{17,16},{24,25},{25,24},{2,3},{3,2... | collective-permute-start | bytes 884744 | tf_op jit(solution)/shard_map/ppermute | solution.py:403
  182.0 20.5 %collective-permute-start.35 = (bf16[72,2048]{1,0:T(8,128)(2,1)}, bf16[72,2048]{1,0:T(8,128)(2,1)S(1)}, u32[]{:S(2)}, u32[]{:S(2)}) collective-permute-start(bf16[72,2048]{1,0:T(8,128)(2,1)} %get-tuple-element.155), channel_id=1, source_target_pairs={{0,8},{1,9},{8,0},{9,1},{16,24},{17,25},{24,16},{25,17},{2,10},{3,... | collective-permute-start | bytes 884744 | tf_op jit(solution)/shard_map/ppermute | solution.py:403
  202.5 22.3 %collective-permute-start.39 = (bf16[72,2048]{1,0:T(8,128)(2,1)}, bf16[72,2048]{1,0:T(8,128)(2,1)}, u32[]{:S(2)}, u32[]{:S(2)}) collective-permute-start(bf16[72,2048]{1,0:T(8,128)(2,1)} %get-tuple-element.159), channel_id=1, source_target_pairs={{0,24},{1,25},{8,16},{9,17},{16,8},{17,9},{24,0},{25,1},{2,26},{3,... | collective-permute-start | bytes 884744 | tf_op jit(solution)/shard_map/ppermute | solution.py:403
  202.5 22.2 %collective-permute-start.40 = (bf16[72,2048]{1,0:T(8,128)(2,1)}, bf16[72,2048]{1,0:T(8,128)(2,1)}, u32[]{:S(2)}, u32[]{:S(2)}) collective-permute-start(bf16[72,2048]{1,0:T(8,128)(2,1)} %get-tuple-element.160), channel_id=1, source_target_pairs={{0,25},{1,24},{8,17},{9,16},{16,9},{17,8},{24,1},{25,0},{2,27},{3,... | collective-permute-start | bytes 884744 | tf_op jit(solution)/shard_map/ppermute | solution.py:403
  207.6 50.1 %collective-permute-start.54 = (bf16[72,2048]{1,0:T(8,128)(2,1)}, bf16[72,2048]{1,0:T(8,128)(2,1)}, u32[]{:S(2)}, u32[]{:S(2)}) collective-permute-start(bf16[72,2048]{1,0:T(8,128)(2,1)} %get-tuple-element.178), channel_id=1, source_target_pairs={{0,9},{1,8},{8,1},{9,0},{16,25},{17,24},{24,17},{25,16},{2,11},{3,... | collective-permute-start | bytes 884744 | tf_op jit(solution)/shard_map/ppermute | solution.py:403
  208.7 51.1 %collective-permute-start.55 = (bf16[72,2048]{1,0:T(8,128)(2,1)}, bf16[72,2048]{1,0:T(8,128)(2,1)}, u32[]{:S(2)}, u32[]{:S(2)}) collective-permute-start(bf16[72,2048]{1,0:T(8,128)(2,1)} %get-tuple-element.180), channel_id=1, source_target_pairs={{0,16},{1,17},{8,24},{9,25},{16,0},{17,1},{24,8},{25,9},{2,18},{3,... | collective-permute-start | bytes 884744 | tf_op jit(solution)/shard_map/ppermute | solution.py:403
  215.7 46.3 %collective-permute-start.56 = (bf16[72,2048]{1,0:T(8,128)(2,1)}, bf16[72,2048]{1,0:T(8,128)(2,1)}, u32[]{:S(2)}, u32[]{:S(2)}) collective-permute-start(bf16[72,2048]{1,0:T(8,128)(2,1)} %get-tuple-element.182), channel_id=1, source_target_pairs={{0,17},{1,16},{8,25},{9,24},{16,1},{17,0},{24,9},{25,8},{2,19},{3,... | collective-permute-start | bytes 884744 | tf_op jit(solution)/shard_map/ppermute | solution.py:403
  224.8 38.8 %collective-permute-start.57 = (bf16[72,2048]{1,0:T(8,128)(2,1)}, bf16[72,2048]{1,0:T(8,128)(2,1)}, u32[]{:S(2)}, u32[]{:S(2)}) collective-permute-start(bf16[72,2048]{1,0:T(8,128)(2,1)} %get-tuple-element.184), channel_id=1, source_target_pairs={{0,24},{1,25},{8,16},{9,17},{16,8},{17,9},{24,0},{25,1},{2,26},{3,... | collective-permute-start | bytes 884744 | tf_op jit(solution)/shard_map/ppermute | solution.py:403
  224.8 39.3 %collective-permute-start.58 = (bf16[72,2048]{1,0:T(8,128)(2,1)}, bf16[72,2048]{1,0:T(8,128)(2,1)}, u32[]{:S(2)}, u32[]{:S(2)}) collective-permute-start(bf16[72,2048]{1,0:T(8,128)(2,1)} %get-tuple-element.186), channel_id=1, source_target_pairs={{0,25},{1,24},{8,17},{9,16},{16,9},{17,8},{24,1},{25,0},{2,27},{3,... | collective-permute-start | bytes 884744 | tf_op jit(solution)/shard_map/ppermute | solution.py:403
  267.6 22.7 %collective-permute-start.73 = (bf16[72,2048]{1,0:T(8,128)(2,1)}, bf16[72,2048]{1,0:T(8,128)(2,1)S(1)}, u32[]{:S(2)}, u32[]{:S(2)}) collective-permute-start(bf16[72,2048]{1,0:T(8,128)(2,1)} %get-tuple-element.200), channel_id=1, source_target_pairs={{0,16},{1,17},{8,24},{9,25},{16,0},{17,1},{24,8},{25,9},{2,18},{3,... | collective-permute-start | bytes 884744 | tf_op jit(solution)/shard_map/ppermute | solution.py:403
  268.7 21.8 %collective-permute-start.74 = (bf16[72,2048]{1,0:T(8,128)(2,1)}, bf16[72,2048]{1,0:T(8,128)(2,1)S(1)}, u32[]{:S(2)}, u32[]{:S(2)}) collective-permute-start(bf16[72,2048]{1,0:T(8,128)(2,1)} %get-tuple-element.201), channel_id=1, source_target_pairs={{0,17},{1,16},{8,25},{9,24},{16,1},{17,0},{24,9},{25,8},{2,19},{3,... | collective-permute-start | bytes 884744 | tf_op jit(solution)/shard_map/ppermute | solution.py:403
  269.2 24.5 %collective-permute-start.75 = (bf16[72,2048]{1,0:T(8,128)(2,1)}, bf16[72,2048]{1,0:T(8,128)(2,1)S(1)}, u32[]{:S(2)}, u32[]{:S(2)}) collective-permute-start(bf16[72,2048]{1,0:T(8,128)(2,1)} %get-tuple-element.202), channel_id=1, source_target_pairs={{0,24},{1,25},{8,16},{9,17},{16,8},{17,9},{24,0},{25,1},{2,26},{3,... | collective-permute-start | bytes 884744 | tf_op jit(solution)/shard_map/ppermute | solution.py:403
  269.2 26.4 %collective-permute-start.76 = (bf16[72,2048]{1,0:T(8,128)(2,1)}, bf16[72,2048]{1,0:T(8,128)(2,1)S(1)}, u32[]{:S(2)}, u32[]{:S(2)}) collective-permute-start(bf16[72,2048]{1,0:T(8,128)(2,1)} %get-tuple-element.203), channel_id=1, source_target_pairs={{0,25},{1,24},{8,17},{9,16},{16,9},{17,8},{24,1},{25,0},{2,27},{3,... | collective-permute-start | bytes 884744 | tf_op jit(solution)/shard_map/ppermute | solution.py:403
  273.4 28.4 %collective-permute-start.61 = (f32[8,128]{1,0:T(8,128)}, f32[8,128]{1,0:T(8,128)S(1)}, u32[]{:S(2)}, u32[]{:S(2)}) collective-permute-start(f32[8,128]{1,0:T(8,128)} %gating.1.gate_ref), channel_id=1, source_target_pairs={{0,6},{2,0},{4,2},{6,4},{1,7},{3,1},{5,3},{7,5},{8,14},{10,8},{12,... | collective-permute-start | bytes 12296 | tf_op jit(solution)/shard_map/ppermute | solution.py:407
  301.8 25.2 %collective-permute-start.77 = (bf16[128,2048]{1,0:T(8,128)(2,1)}, bf16[128,2048]{1,0:T(8,128)(2,1)S(1)}, u32[]{:S(2)}, u32[]{:S(2)}) collective-permute-start(bf16[128,2048]{1,0:T(8,128)(2,1)} %get-tuple-element.204), channel_id=1, source_target_pairs={{0,2},{2,4},{4,6},{6,0},{1,3},{3,5},{5,7},{7,1},{8,10},{10,12},{12... | collective-permute-start | bytes 1572872 | tf_op jit(solution)/shard_map/ppermute | solution.py:407
  303.4 30.2 %collective-permute-start.79 = (bf16[128,2048]{1,0:T(8,128)(2,1)}, bf16[128,2048]{1,0:T(8,128)(2,1)}, u32[]{:S(2)}, u32[]{:S(2)}) collective-permute-start(bf16[128,2048]{1,0:T(8,128)(2,1)} %get-tuple-element.205), channel_id=1, source_target_pairs={{0,2},{2,4},{4,6},{6,0},{1,3},{3,5},{5,7},{7,1},{8,10},{10,12},{12... | collective-permute-start | bytes 1572872 | tf_op jit(solution)/shard_map/ppermute | solution.py:407
  304.6 21.2 %collective-permute-start.67 = (bf16[72,2048]{1,0:T(8,128)(2,1)}, bf16[72,2048]{1,0:T(8,128)(2,1)S(1)}, u32[]{:S(2)}, u32[]{:S(2)}) collective-permute-start(bf16[72,2048]{1,0:T(8,128)(2,1)} %get-tuple-element.194), channel_id=1, source_target_pairs={{0,24},{1,25},{8,16},{9,17},{16,8},{17,9},{24,0},{25,1},{2,26},{3,... | collective-permute-start | bytes 884744 | tf_op jit(solution)/shard_map/ppermute | solution.py:403
  305.7 20.3 %collective-permute-start.68 = (bf16[72,2048]{1,0:T(8,128)(2,1)}, bf16[72,2048]{1,0:T(8,128)(2,1)S(1)}, u32[]{:S(2)}, u32[]{:S(2)}) collective-permute-start(bf16[72,2048]{1,0:T(8,128)(2,1)} %get-tuple-element.195), channel_id=1, source_target_pairs={{0,25},{1,24},{8,17},{9,16},{16,9},{17,8},{24,1},{25,0},{2,27},{3,... | collective-permute-start | bytes 884744 | tf_op jit(solution)/shard_map/ppermute | solution.py:403
  315.1 26.2 %collective-permute-start.45 = (bf16[72,2048]{1,0:T(8,128)(2,1)}, bf16[72,2048]{1,0:T(8,128)(2,1)}, u32[]{:S(2)}, u32[]{:S(2)}) collective-permute-start(bf16[72,2048]{1,0:T(8,128)(2,1)} %get-tuple-element.165), channel_id=1, source_target_pairs={{0,8},{1,9},{8,0},{9,1},{16,24},{17,25},{24,16},{25,17},{2,10},{3,... | collective-permute-start | bytes 884744 | tf_op jit(solution)/shard_map/ppermute | solution.py:403
  327.0 19.5 %collective-permute-start.48 = (bf16[72,2048]{1,0:T(8,128)(2,1)}, bf16[72,2048]{1,0:T(8,128)(2,1)}, u32[]{:S(2)}, u32[]{:S(2)}) collective-permute-start(bf16[72,2048]{1,0:T(8,128)(2,1)} %get-tuple-element.168), channel_id=1, source_target_pairs={{0,17},{1,16},{8,25},{9,24},{16,1},{17,0},{24,9},{25,8},{2,19},{3,... | collective-permute-start | bytes 884744 | tf_op jit(solution)/shard_map/ppermute | solution.py:403
  344.5 23.9 %collective-permute-start.60 = (bf16[128,2048]{1,0:T(8,128)(2,1)}, bf16[128,2048]{1,0:T(8,128)(2,1)S(1)}, u32[]{:S(2)}, u32[]{:S(2)}) collective-permute-start(bf16[128,2048]{1,0:T(8,128)(2,1)} %get-tuple-element.188), channel_id=1, source_target_pairs={{0,6},{2,0},{4,2},{6,4},{1,7},{3,1},{5,3},{7,5},{8,14},{10,8},{12,... | collective-permute-start | bytes 1572872 | tf_op jit(solution)/shard_map/ppermute | solution.py:407
  345.4 35.4 %collective-permute-start.78 = (bf16[128,2048]{1,0:T(8,128)(2,1)}, bf16[128,2048]{1,0:T(8,128)(2,1)S(1)}, u32[]{:S(2)}, u32[]{:S(2)}) collective-permute-start(bf16[128,2048]{1,0:T(8,128)(2,1)} %combine.7), channel_id=1, source_target_pairs={{0,2},{2,4},{4,6},{6,0},{1,3},{3,5},{5,7},{7,1},{8,10},{10,12},{12... | collective-permute-start | bytes 1572872 | tf_op jit(solution)/shard_map/ppermute | solution.py:407
  346.5 45.3 %collective-permute-start.80 = (bf16[128,2048]{1,0:T(8,128)(2,1)}, bf16[128,2048]{1,0:T(8,128)(2,1)S(1)}, u32[]{:S(2)}, u32[]{:S(2)}) collective-permute-start(bf16[128,2048]{1,0:T(8,128)(2,1)} %combine.8), channel_id=1, source_target_pairs={{0,2},{2,4},{4,6},{6,0},{1,3},{3,5},{5,7},{7,1},{8,10},{10,12},{12... | collective-permute-start | bytes 1572872 | tf_op jit(solution)/shard_map/ppermute | solution.py:407
  (100 other events, 2364.7 us)
where the time goes:
time: 399 us; the launch traced here: 398 us
  waiting for transfers between devices  182 us (46%)
  Pallas kernels  106 us (27%)
  starting transfers between devices  92.2 us (23%)
  local copies, waits for them, and re-layouts  7.34 us (2%)
  other arithmetic  6.66 us (2%)
    ppermute x63, waiting for transfers between devices, cross(): lax.ppermute(value, axis, [(i, i ^ k) for i in range(n)])  121 us
    pallas_call x3, Pallas kernels, ffn(): pl.pallas_call(functools.partial(ffn_kernel, n, exp_dev, low, high), grid...  64.4 us
    ppermute x18, waiting for transfers between devices, shift(): return lax.ppermute(value, 'plane', pairs) if s % n_plane else value  61.9 us
    ppermute x63, starting transfers between devices, cross(): lax.ppermute(value, axis, [(i, i ^ k) for i in range(n)])  55 us
    ppermute x18, starting transfers between devices, shift(): return lax.ppermute(value, 'plane', pairs) if s % n_plane else value  37.1 us
    pallas_call x5, Pallas kernels, combine(): pl.pallas_call(functools.partial(combine_kernel, exp_dev, n, halves, join...  21.4 us
    pallas_call x4, Pallas kernels, pack(): pl.pallas_call(functools.partial(pack_kernel, exp_dev), out_shape=[jax.Sh...  13.7 us
  transfers between devices with their start and end apart: 81, of which 27 were waited for; matrix products, arithmetic and copies ran while one was open for 3% of the time, Pallas kernels for 25%

commit v1 on v0

--- a/solution.py
+++ b/solution.py
@@ -406,9 +406,6 @@
         pairs = [(i, (i + s) % n_plane) for i in range(n_plane)]
         return lax.ppermute(value, "plane", pairs) if s % n_plane else value
 
-    def after(value, *deps):
-        return lax.optimization_barrier((value, *deps))[0]
-
     peers = [peer ^ k for k in range(n_peer)]
     dst = jnp.stack([((p // n_side) * n_plane + plane) * n_side + p % n_side for p in peers])
     dst = dst.astype(jnp.int32)
@@ -433,10 +430,10 @@
         slots[s] = shift(slot_t, s)
 
     def send(pieces):
-        out = []
-        for k in range(n_peer):
-            out.append(cross(pieces[k], k, PLANE, n_peer))
-        return out
+        out = {}
+        for k in reversed(range(n_peer)):
+            out[k] = cross(pieces[k], k, PLANE, n_peer)
+        return [out[k] for k in range(n_peer)]
 
     def packed(s):
         return pack(exp_dev, dst, slots[s], toks[s])
@@ -456,9 +453,7 @@
     sent[0] = packed(0)
     came[0] = send(sent[0])
 
-    logits = jnp.dot(
-        tokens, after(router_weight, sent[0][0]), preferred_element_type=jnp.float32
-    )
+    logits = jnp.dot(tokens, router_weight, preferred_element_type=jnp.float32)
     scores = jnp.exp(logits).T
     pad = round_up(n_group, 8)
     sums = jnp.pad(jnp.sum(scores.reshape(n_group, size, count), 1), ((0, pad - n_group), (0, 0)))
@@ -467,15 +462,23 @@
         part = lax.dynamic_slice_in_dim(scores, (group ^ k) * size, size, 0)
         held.append(cross(jnp.concatenate([part, sums], 0), k, "group", n_group))
 
-    last = None
     for s in pairs[0][1:]:
         sent[s] = packed(s)
         came[s] = send(sent[s])
-        last = sent[s][0]
-    if last is not None:
-        held = [after(h, last) for h in held]
     held = jnp.stack(held)
     held = jnp.concatenate([held] + [cross(held, k, "side", n_side) for k in range(1, n_side)], 0)
+    gcap = group_capacity.astype(jnp.float32)
+    gtarget = count * devices * gcap / jnp.sum(gcap)
+    ecap = expert_capacity.astype(jnp.float32).reshape(n_group, size)
+    etarget = (gtarget / jnp.sum(ecap, 1))[:, None] * ecap
+    own_target = lax.dynamic_index_in_dim(etarget, group, 0, keepdims=False)
+    held, gtarget, own_target = lax.optimization_barrier(
+        (
+            held,
+            jnp.broadcast_to(gtarget[:, None], (n_group, count)),
+            jnp.broadcast_to(own_target[:, None], (size, count)),
+        )
+    )
     for s in shifts:
         if s not in sent and s in (pairs + [[]])[1]:
             sent[s] = packed(s)
@@ -489,11 +492,6 @@
             sent[s] = packed(s)
             came[s] = send(sent[s])
 
-    gcap = group_capacity.astype(jnp.float32)
-    gtarget = count * devices * gcap / jnp.sum(gcap)
-    ecap = expert_capacity.astype(jnp.float32).reshape(n_group, size)
-    etarget = (gtarget / jnp.sum(ecap, 1))[:, None] * ecap
-    own_target = lax.dynamic_index_in_dim(etarget, group, 0, keepdims=False)
     plan, fac = pl.pallas_call(
         functools.partial(balance_kernel, n_group, size),
         out_shape=[
@@ -511,9 +509,9 @@
         name="balance",
     )(
         group.astype(jnp.int32)[None],
-        after(sums, made[0][0]),
-        jnp.broadcast_to(gtarget[:, None], (n_group, count)),
-        jnp.broadcast_to(own_target[:, None], (size, count)),
+        sums,
+        gtarget,
+        own_target,
         *spread,
     )
     facs = []
@@ -522,7 +520,7 @@
 
     early = [s for s in pairs[0] if s]
     for s in early:
-        back[s] = send([after(p, plan) for p in made[s]])
+        back[s] = send(made[s])
     for i in range(1, len(pairs)):
         made.update(feed(i))
     late = [s for group_of in pairs[1:] for s in group_of][::-1]
@@ -539,7 +537,7 @@
     )(
         jnp.stack([group ^ k for k in range(n_group)]).astype(jnp.int32),
         scores,
-        after(plan, made[late[-1]][0]) if late else plan,
+        plan,
         dest_t,
         *facs,
     )

time: 399 us -> 426 us (1.068)
  waiting for transfers between devices: 182 us -> 220 us
  starting transfers between devices: 92.2 us -> 84.6 us
    ppermute x18, waiting for transfers between devices: 61.9 us -> 102 us  [shift(): return lax.ppermute(value, 'plane', pairs) if s % n_plane else value]
    ppermute x18, starting transfers between devices: 37.1 us -> 24.3 us  [shift(): return lax.ppermute(value, 'plane', pairs) if s % n_plane else value]
    ppermute x63, starting transfers between devices: 55 us -> 60.3 us  [cross(): lax.ppermute(value, axis, [(i, i ^ k) for i in range(n)])]
  transfers between devices with their start and end apart: 81 -> 81, of which waited for: 27 -> 32; matrix products, arithmetic and copies ran while one was open for 3% -> 2% of each run, Pallas kernels for 25% -> 24%
where the time goes in v1:
time: 426 us; the launch traced here: 425 us
  waiting for transfers between devices  220 us (52%)
  Pallas kernels  106 us (25%)
  starting transfers between devices  84.6 us (20%)
  local copies, waits for them, and re-layouts  6.45 us (2%)
  other arithmetic  5.35 us (1%)
    ppermute x63, waiting for transfers between devices, cross(): lax.ppermute(value, axis, [(i, i ^ k) for i in range(n)])  118 us
    ppermute x18, waiting for transfers between devices, shift(): return lax.ppermute(value, 'plane', pairs) if s % n_plane else value  102 us
    pallas_call x3, Pallas kernels, ffn(): pl.pallas_call(functools.partial(ffn_kernel, n, exp_dev, low, high), grid...  64.5 us
    ppermute x63, starting transfers between devices, cross(): lax.ppermute(value, axis, [(i, i ^ k) for i in range(n)])  60.3 us
    ppermute x18, starting transfers between devices, shift(): return lax.ppermute(value, 'plane', pairs) if s % n_plane else value  24.3 us
    pallas_call x5, Pallas kernels, combine(): pl.pallas_call(functools.partial(combine_kernel, exp_dev, n, halves, join...  21.3 us
    pallas_call x4, Pallas kernels, pack(): pl.pallas_call(functools.partial(pack_kernel, exp_dev), out_shape=[jax.Sh...  13.4 us
  transfers between devices with their start and end apart: 81, of which 32 were waited for; matrix products, arithmetic and copies ran while one was open for 2% of the time, Pallas kernels for 24%

profile of v1, /device:TPU:0, one launch (start us, length us, event | category | flops | bytes accessed | tf_op | source)
XLA Modules:
  0.0 425.2 jit_solution(1048987303859162983)
XLA Ops:
  0.6 3.1 collective-permute-start.18
  3.8 2.1 collective-permute-start.45
  16.6 3.1 collective-permute-done.3
  21.7 2.5 collective-permute-start.53
  25.5 29.1 %collective-permute-done.53.slot_ref = s32[8,128]{1,0:T(8,128)S(1)} collective-permute-done((s32[8,128]{1,0:T(8,128)S(1)}, s32[8,128]{1,0:T(8,128)S(1)}, u32[]{:S(2)}, u32[]{:S(2)}) %collective-permute-start.53) | collective-permute-done | bytes 4128 | tf_op jit(solution)/shard_map/ppermute | solution.py:407
  54.6 5.8 %collective-permute-start.43 = (s32[8,128]{1,0:T(8,128)S(1)}, s32[8,128]{1,0:T(8,128)S(1)}, u32[]{:S(2)}, u32[]{:S(2)}) collective-permute-start(s32[8,128]{1,0:T(8,128)S(1)} %bitcast_add_fusion.slot_ref), channel_id=1, source_target_pairs={{0,6},{2,0},{4,2},{6,4},{1,7},{3,1},{5,3},{7,5},{8,14},{10,8},{12,... | collective-permute-start | bytes 12296 | tf_op jit(solution)/shard_map/ppermute | solution.py:407
  61.8 3.3 pack.4
  65.2 2.3 collective-permute-done.17.slot_ref
  69.0 2.5 collective-permute-start.6
  71.7 30.2 %collective-permute-done.6.refs_3_ = f32[8,40,128]{2,1,0:T(8,128)S(1)} collective-permute-done((f32[8,40,128]{2,1,0:T(8,128)S(1)}, f32[8,40,128]{2,1,0:T(8,128)S(1)}, u32[]{:S(2)}, u32[]{:S(2)}) %collective-permute-start.6) | collective-permute-done | bytes 163872 | tf_op jit(solution)/shard_map/ppermute | solution.py:407
  105.1 4.9 %balance.1 = (f32[8,128]{1,0:T(8,128)}, f32[64,128]{1,0:T(8,128)}) custom-call(s32[1]{0:T(128)} %bitcast.10.mine_ref, f32[8,128]{1,0:T(8,128)} %copy-done.47, f32[4,128]{1,0:T(4,128)} %broadcast_in_dim.20.gt_ref, f32[32,128]{1,0:T(8,128)} %broadcast_in_dim.22.et_ref, f32[8,40,128]{2,1,0:T(8,128)} %copy-done.43, f32[8,40,128]{2,1,0:T(8,128)} %copy-done.44, ...), custom_call_target="tpu_custom_call" | custom-call | flops 10485760 | bytes 524288 | tf_op jit(solution)/shard_map/balance/pallas_call | solution.py:495
  111.8 5.4 %collective-permute-done.13.refs_4_.refs_20_ = bf16[72,2048]{1,0:T(8,128)(2,1)S(1)} collective-permute-done((bf16[72,2048]{1,0:T(8,128)(2,1)}, bf16[72,2048]{1,0:T(8,128)(2,1)S(1)}, u32[]{:S(2)}, u32[]{:S(2)}) %collective-permute-start.13) | collective-permute-done | bytes 294944 | tf_op jit(solution)/shard_map/ppermute | solution.py:403
  118.7 2.0 collective-permute-start.16
  123.2 3.3 pack.6
  126.5 7.5 %collective-permute-done.8.refs_2_ = f32[64,128]{1,0:T(8,128)S(1)} collective-permute-done((f32[64,128]{1,0:T(8,128)}, f32[64,128]{1,0:T(8,128)S(1)}, u32[]{:S(2)}, u32[]{:S(2)}) %collective-permute-start.8) | collective-permute-done | bytes 32800 | tf_op jit(solution)/shard_map/ppermute | solution.py:403
  134.0 2.0 collective-permute-start.46
  138.5 4.7 %collective-permute-done.69.gate_ref = f32[8,128]{1,0:T(8,128)} collective-permute-done((f32[8,128]{1,0:T(8,128)}, f32[8,128]{1,0:T(8,128)}, u32[]{:S(2)}, u32[]{:S(2)}) %collective-permute-start.69) | collective-permute-done | bytes 4128 | tf_op jit(solution)/shard_map/ppermute | solution.py:407
  143.2 3.3 pack.5
  146.6 2.2 collective-permute-done.33.gate_ref
  152.2 3.9 collective-permute-done.48.refs_3_.refs_19_
  157.7 3.7 collective-permute-done.19.refs_9_.refs_25_
  165.2 3.4 pack.7
  168.7 1.9 collective-permute-start.50
  171.2 3.4 collective-permute-done.23.refs_13_.refs_29_
  176.2 20.9 %collective-permute-done.24.refs_14_.refs_30_ = bf16[72,2048]{1,0:T(8,128)(2,1)S(1)} collective-permute-done((bf16[72,2048]{1,0:T(8,128)(2,1)}, bf16[72,2048]{1,0:T(8,128)(2,1)S(1)}, u32[]{:S(2)}, u32[]{:S(2)}) %collective-permute-start.24) | collective-permute-done | bytes 294944 | tf_op jit(solution)/shard_map/ppermute | solution.py:403
  199.7 16.3 %ffn.3 = (bf16[72,2048]{1,0:T(8,128)(2,1)}, bf16[72,2048]{1,0:T(8,128)(2,1)}, bf16[72,2048]{1,0:T(8,128)(2,1)}, bf16[72,2048]{1,0:T(8,128)(2,1)}, bf16[72,2048]{...) custom-call(bf16[72,2048]{1,0:T(8,128)(2,1)} %get-tuple-element.97.r, ...), custom_call_target="tpu_custom_call" | custom-call | flops 5435817984 | bytes 47185920 | tf_op jit(solution)/shard_map/ffn/pallas_call | solution.py:226
  219.8 2.0 collective-permute-start.61
  221.8 16.5 %ffn.4 = (bf16[72,2048]{1,0:T(8,128)(2,1)}, bf16[72,2048]{1,0:T(8,128)(2,1)}, bf16[72,2048]{1,0:T(8,128)(2,1)}, bf16[72,2048]{1,0:T(8,128)(2,1)}, bf16[72,2048]{...) custom-call(bf16[72,2048]{1,0:T(8,128)(2,1)} %get-tuple-element.97.r, ...), custom_call_target="tpu_custom_call", output_to_operand_aliasing={{0}: (36, {}), {1}: (37, {}), {2}: (38, {}), {3}: (39, {}),... | custom-call | flops 5435817984 | bytes 47185920 | tf_op jit(solution)/shard_map/ffn/pallas_call | solution.py:226
  241.1 3.2 collective-permute-done.60.refs_14_.refs_30_
  246.9 31.8 %ffn.5 = (bf16[72,2048]{1,0:T(8,128)(2,1)}, bf16[72,2048]{1,0:T(8,128)(2,1)}, bf16[72,2048]{1,0:T(8,128)(2,1)}, bf16[72,2048]{1,0:T(8,128)(2,1)}, bf16[72,2048]{...) custom-call(bf16[72,2048]{1,0:T(8,128)(2,1)} %get-tuple-element.148., ...), custom_call_target="tpu_custom_call" | custom-call | flops 10871635968 | bytes 84934656 | tf_op jit(solution)/shard_map/ffn/pallas_call | solution.py:226
  283.0 10.7 %collective-permute-done.39.refs_6_ = bf16[72,2048]{1,0:T(8,128)(2,1)S(1)} collective-permute-done((bf16[72,2048]{1,0:T(8,128)(2,1)S(1)}, bf16[72,2048]{1,0:T(8,128)(2,1)S(1)}, u32[]{:S(2)}, u32[]{:S(2)}) %collective-permute-start.39) | collective-permute-done | bytes 294944 | tf_op jit(solution)/shard_map/ppermute | solution.py:403
  298.4 3.7 collective-permute-done.72.refs_3_
  303.2 13.3 %collective-permute-done.73.refs_4_ = bf16[72,2048]{1,0:T(8,128)(2,1)S(1)} collective-permute-done((bf16[72,2048]{1,0:T(8,128)(2,1)}, bf16[72,2048]{1,0:T(8,128)(2,1)S(1)}, u32[]{:S(2)}, u32[]{:S(2)}) %collective-permute-start.73) | collective-permute-done | bytes 294944 | tf_op jit(solution)/shard_map/ppermute | solution.py:403
  317.5 5.0 %collective-permute-done.75.refs_6_ = bf16[72,2048]{1,0:T(8,128)(2,1)S(1)} collective-permute-done((bf16[72,2048]{1,0:T(8,128)(2,1)}, bf16[72,2048]{1,0:T(8,128)(2,1)S(1)}, u32[]{:S(2)}, u32[]{:S(2)}) %collective-permute-start.75) | collective-permute-done | bytes 294944 | tf_op jit(solution)/shard_map/ppermute | solution.py:403
  324.6 4.4 %combine.6 = (bf16[128,2048]{1,0:T(8,128)(2,1)}, bf16[128,2048]{1,0:T(8,128)(2,1)}) custom-call(s32[8]{0:T(128)} %stack.65.dst_ref, s32[8,128]{1,0:T(8,128)} %copy-done.65, f32[8,128]{1,0:T(8,128)} %collective-permute-done.69.gate_ref, bf16[72,2048]{1,0:T(8,128)(2,1)} %get-tuple-element.172.refs_0_, bf16[72,2048]{1,0:T(8,128)(2,1)} %copy-done.58, ...), custom_call_target="tpu_custom_call" | custom-call | flops 1207959552 | bytes 3407872 | tf_op jit(solution)/shard_map/combine/pallas_call | solution.py:306
  331.2 2.6 collective-permute-done.64.refs_3_
  335.9 5.1 %collective-permute-done.66.refs_5_ = bf16[72,2048]{1,0:T(8,128)(2,1)S(1)} collective-permute-done((bf16[72,2048]{1,0:T(8,128)(2,1)}, bf16[72,2048]{1,0:T(8,128)(2,1)S(1)}, u32[]{:S(2)}, u32[]{:S(2)}) %collective-permute-start.66) | collective-permute-done | bytes 294944 | tf_op jit(solution)/shard_map/ppermute | solution.py:403
  341.1 12.3 %collective-permute-done.67.refs_6_ = bf16[72,2048]{1,0:T(8,128)(2,1)S(1)} collective-permute-done((bf16[72,2048]{1,0:T(8,128)(2,1)}, bf16[72,2048]{1,0:T(8,128)(2,1)S(1)}, u32[]{:S(2)}, u32[]{:S(2)}) %collective-permute-start.67) | collective-permute-done | bytes 294944 | tf_op jit(solution)/shard_map/ppermute | solution.py:403
  356.8 4.4 %combine.5 = (bf16[128,2048]{1,0:T(8,128)(2,1)}, bf16[128,2048]{1,0:T(8,128)(2,1)}) custom-call(s32[8]{0:T(128)} %stack.65.dst_ref, s32[8,128]{1,0:T(8,128)} %copy-done.66, f32[8,128]{1,0:T(8,128)} %copy-done.67, bf16[72,2048]{1,0:T(8,128)(2,1)} %get-tuple-element.138.refs_0_, bf16[72,2048]{1,0:T(8,128)(2,1)} %copy-done.55, ...), custom_call_target="tpu_custom_call" | custom-call | flops 1207959552 | bytes 3407872 | tf_op jit(solution)/shard_map/combine/pallas_call | solution.py:306
  361.6 3.6 combine.8
  365.2 3.7 combine.7
  368.8 3.8 collective-permute-start.41
  372.7 2.0 collective-permute-start.80
  377.4 8.9 %collective-permute-done.32.refs_7_ = bf16[72,2048]{1,0:T(8,128)(2,1)S(1)} collective-permute-done((bf16[72,2048]{1,0:T(8,128)(2,1)}, bf16[72,2048]{1,0:T(8,128)(2,1)S(1)}, u32[]{:S(2)}, u32[]{:S(2)}) %collective-permute-start.32) | collective-permute-done | bytes 294944 | tf_op jit(solution)/shard_map/ppermute | solution.py:403
  386.3 10.2 %collective-permute-done.42.refs_9_ = bf16[128,2048]{1,0:T(8,128)(2,1)S(1)} collective-permute-done((bf16[128,2048]{1,0:T(8,128)(2,1)}, bf16[128,2048]{1,0:T(8,128)(2,1)S(1)}, u32[]{:S(2)}, u32[]{:S(2)}) %collective-permute-start.42) | collective-permute-done | bytes 524320 | tf_op jit(solution)/shard_map/ppermute | solution.py:407
  396.5 11.5 %collective-permute-done.80.refs_11_ = bf16[128,2048]{1,0:T(8,128)(2,1)S(1)} collective-permute-done((bf16[128,2048]{1,0:T(8,128)(2,1)}, bf16[128,2048]{1,0:T(8,128)(2,1)S(1)}, u32[]{:S(2)}, u32[]{:S(2)}) %collective-permute-start.80) | collective-permute-done | bytes 524320 | tf_op jit(solution)/shard_map/ppermute | solution.py:407
  408.0 11.2 %collective-permute-done.78.refs_10_ = bf16[128,2048]{1,0:T(8,128)(2,1)S(1)} collective-permute-done((bf16[128,2048]{1,0:T(8,128)(2,1)}, bf16[128,2048]{1,0:T(8,128)(2,1)S(1)}, u32[]{:S(2)}, u32[]{:S(2)}) %collective-permute-start.78) | collective-permute-done | bytes 524320 | tf_op jit(solution)/shard_map/ppermute | solution.py:407
  420.1 5.2 %combine.9 = bf16[128,4096]{1,0:T(8,128)(2,1)} custom-call(s32[8]{0:T(128)} %stack.65.dst_ref, s32[8,128]{1,0:T(8,128)} %copy-done.53, f32[8,128]{1,0:T(8,128)} %gating.1.gate_ref, bf16[72,2048]{1,0:T(8,128)(2,1)} %get-tuple-element.130.refs_0_, bf16[72,2048]{1,0:T(8,128)(2,1)} %copy-done.41, bf16[72,2048]{1,0:T(8,128)(2,1)} %collective-permute-done.27.refs_2_, ...), custom_call_target="tpu_custom_call" | custom-call | flops 1207959552 | bytes 5505024 | tf_op jit(solution)/shard_map/combine/pallas_call | solution.py:306
  (291 shorter events, 75.9 us)
Async XLA Ops:
  0.6 70.8 %collective-permute-start.18 = (bf16[128,4096]{1,0:T(8,128)(2,1)}, bf16[128,4096]{1,0:T(8,128)(2,1)}, u32[]{:S(2)}, u32[]{:S(2)}) collective-permute-start(bf16[128,4096]{1,0:T(8,128)(2,1)} %tok_ref.1), channel_id=1, source_target_pairs={{0,2},{2,4},{4,6},{6,0},{1,3},{3,5},{5,7},{7,1},{8,10},{10,12},{12... | collective-permute-start | bytes 3145736 | tf_op jit(solution)/shard_map/ppermute | solution.py:407
  3.8 118.4 %collective-permute-start.45 = (bf16[128,4096]{1,0:T(8,128)(2,1)}, bf16[128,4096]{1,0:T(8,128)(2,1)S(1)}, u32[]{:S(2)}, u32[]{:S(2)}) collective-permute-start(bf16[128,4096]{1,0:T(8,128)(2,1)} %tok_ref.1), channel_id=1, source_target_pairs={{0,6},{2,0},{4,2},{6,4},{1,7},{3,1},{5,3},{7,5},{8,14},{10,8},{12,... | collective-permute-start | bytes 3145736 | tf_op jit(solution)/shard_map/ppermute | solution.py:407
  21.0 48.0 %collective-permute-start.4 = (f32[8,40,128]{2,1,0:T(8,128)S(1)}, f32[8,40,128]{2,1,0:T(8,128)S(1)}, u32[]{:S(2)}, u32[]{:S(2)}) collective-permute-start(f32[8,40,128]{2,1,0:T(8,128)S(1)} %constant_dynamic-update-slice_fusion.refs_0_), channel_id=1, source_target_pairs={{0,2},{2,4},{4,6},{6,0},{1,3},{3,5},{5,7},{7,1},{8,10},{10,12},{12... | collective-permute-start | bytes 491528 | tf_op jit(solution)/shard_map/ppermute | solution.py:407
  21.7 33.0 %collective-permute-start.53 = (s32[8,128]{1,0:T(8,128)S(1)}, s32[8,128]{1,0:T(8,128)S(1)}, u32[]{:S(2)}, u32[]{:S(2)}) collective-permute-start(s32[8,128]{1,0:T(8,128)S(1)} %bitcast_add_fusion.slot_ref), channel_id=1, source_target_pairs={{0,4},{2,6},{4,0},{6,2},{1,5},{3,7},{5,1},{7,3},{8,12},{10,14},{12... | collective-permute-start | bytes 12296 | tf_op jit(solution)/shard_map/ppermute | solution.py:407
  24.2 44.8 %collective-permute-start.5 = (f32[8,40,128]{2,1,0:T(8,128)S(1)}, f32[8,40,128]{2,1,0:T(8,128)S(1)}, u32[]{:S(2)}, u32[]{:S(2)}) collective-permute-start(f32[8,40,128]{2,1,0:T(8,128)S(1)} %constant_dynamic-update-slice_fusion.refs_0_), channel_id=1, source_target_pairs={{0,6},{2,0},{4,2},{6,4},{1,7},{3,1},{5,3},{7,5},{8,14},{10,8},{12,... | collective-permute-start | bytes 491528 | tf_op jit(solution)/shard_map/ppermute | solution.py:407
  67.5 34.6 %collective-permute-start.10 = (bf16[72,2048]{1,0:T(8,128)(2,1)}, bf16[72,2048]{1,0:T(8,128)(2,1)S(1)}, u32[]{:S(2)}, u32[]{:S(2)}) collective-permute-start(bf16[72,2048]{1,0:T(8,128)(2,1)} %get-tuple-element.98), channel_id=1, source_target_pairs={{0,1},{1,0},{8,9},{9,8},{16,17},{17,16},{24,25},{25,24},{2,3},{3,2... | collective-permute-start | bytes 884744 | tf_op jit(solution)/shard_map/ppermute | solution.py:403
  69.0 34.6 %collective-permute-start.11 = (bf16[72,2048]{1,0:T(8,128)(2,1)}, bf16[72,2048]{1,0:T(8,128)(2,1)S(1)}, u32[]{:S(2)}, u32[]{:S(2)}) collective-permute-start(bf16[72,2048]{1,0:T(8,128)(2,1)} %get-tuple-element.99), channel_id=1, source_target_pairs={{0,8},{1,9},{8,0},{9,1},{16,24},{17,25},{24,16},{25,17},{2,10},{3,... | collective-permute-start | bytes 884744 | tf_op jit(solution)/shard_map/ppermute | solution.py:403
  69.0 32.9 %collective-permute-start.6 = (f32[8,40,128]{2,1,0:T(8,128)S(1)}, f32[8,40,128]{2,1,0:T(8,128)S(1)}, u32[]{:S(2)}, u32[]{:S(2)}) collective-permute-start(f32[8,40,128]{2,1,0:T(8,128)S(1)} %constant_dynamic-update-slice_fusion.refs_0_), channel_id=1, source_target_pairs={{0,4},{2,6},{4,0},{6,2},{1,5},{3,7},{5,1},{7,3},{8,12},{10,14},{12... | collective-permute-start | bytes 491528 | tf_op jit(solution)/shard_map/ppermute | solution.py:407
  71.5 92.5 %collective-permute-start.54 = (bf16[128,4096]{1,0:T(8,128)(2,1)}, bf16[128,4096]{1,0:T(8,128)(2,1)}, u32[]{:S(2)}, u32[]{:S(2)}) collective-permute-start(bf16[128,4096]{1,0:T(8,128)(2,1)} %collective-permute-done.18.tok_ref), channel_id=1, source_target_pairs={{0,2},{2,4},{4,6},{6,0},{1,3},{3,5},{5,7},{7,1},{8,10},{10,12},{12... | collective-permute-start | bytes 3145736 | tf_op jit(solution)/shard_map/ppermute | solution.py:407
  117.1 21.1 %collective-permute-start.15 = (bf16[72,2048]{1,0:T(8,128)(2,1)}, bf16[72,2048]{1,0:T(8,128)(2,1)S(1)}, u32[]{:S(2)}, u32[]{:S(2)}) collective-permute-start(bf16[72,2048]{1,0:T(8,128)(2,1)} %get-tuple-element.103), channel_id=1, source_target_pairs={{0,24},{1,25},{8,16},{9,17},{16,8},{17,9},{24,0},{25,1},{2,26},{3,... | collective-permute-start | bytes 884744 | tf_op jit(solution)/shard_map/ppermute | solution.py:403
  118.7 19.7 %collective-permute-start.16 = (bf16[72,2048]{1,0:T(8,128)(2,1)}, bf16[72,2048]{1,0:T(8,128)(2,1)S(1)}, u32[]{:S(2)}, u32[]{:S(2)}) collective-permute-start(bf16[72,2048]{1,0:T(8,128)(2,1)} %get-tuple-element.104), channel_id=1, source_target_pairs={{0,25},{1,24},{8,17},{9,16},{16,9},{17,8},{24,1},{25,0},{2,27},{3,... | collective-permute-start | bytes 884744 | tf_op jit(solution)/shard_map/ppermute | solution.py:403
  134.0 15.7 %collective-permute-start.46 = (bf16[72,2048]{1,0:T(8,128)(2,1)}, bf16[72,2048]{1,0:T(8,128)(2,1)S(1)}, u32[]{:S(2)}, u32[]{:S(2)}) collective-permute-start(bf16[72,2048]{1,0:T(8,128)(2,1)} %get-tuple-element.149), channel_id=1, source_target_pairs={{0,1},{1,0},{8,9},{9,8},{16,17},{17,16},{24,25},{25,24},{2,3},{3,2... | collective-permute-start | bytes 884744 | tf_op jit(solution)/shard_map/ppermute | solution.py:403
  136.1 15.4 %collective-permute-start.47 = (bf16[72,2048]{1,0:T(8,128)(2,1)}, bf16[72,2048]{1,0:T(8,128)(2,1)S(1)}, u32[]{:S(2)}, u32[]{:S(2)}) collective-permute-start(bf16[72,2048]{1,0:T(8,128)(2,1)} %get-tuple-element.150), channel_id=1, source_target_pairs={{0,8},{1,9},{8,0},{9,1},{16,24},{17,25},{24,16},{25,17},{2,10},{3,... | collective-permute-start | bytes 884744 | tf_op jit(solution)/shard_map/ppermute | solution.py:403
  163.1 34.1 %collective-permute-start.24 = (bf16[72,2048]{1,0:T(8,128)(2,1)}, bf16[72,2048]{1,0:T(8,128)(2,1)S(1)}, u32[]{:S(2)}, u32[]{:S(2)}) collective-permute-start(bf16[72,2048]{1,0:T(8,128)(2,1)} %get-tuple-element.111), channel_id=1, source_target_pairs={{0,24},{1,25},{8,16},{9,17},{16,8},{17,9},{24,0},{25,1},{2,26},{3,... | collective-permute-start | bytes 884744 | tf_op jit(solution)/shard_map/ppermute | solution.py:403
  164.0 34.4 %collective-permute-start.25 = (bf16[72,2048]{1,0:T(8,128)(2,1)}, bf16[72,2048]{1,0:T(8,128)(2,1)S(1)}, u32[]{:S(2)}, u32[]{:S(2)}) collective-permute-start(bf16[72,2048]{1,0:T(8,128)(2,1)} %get-tuple-element.112), channel_id=1, source_target_pairs={{0,25},{1,24},{8,17},{9,16},{16,9},{17,8},{24,1},{25,0},{2,27},{3,... | collective-permute-start | bytes 884744 | tf_op jit(solution)/shard_map/ppermute | solution.py:403
  168.7 47.3 %collective-permute-start.50 = (bf16[72,2048]{1,0:T(8,128)(2,1)}, bf16[72,2048]{1,0:T(8,128)(2,1)}, u32[]{:S(2)}, u32[]{:S(2)}) collective-permute-start(bf16[72,2048]{1,0:T(8,128)(2,1)} %get-tuple-element.153), channel_id=1, source_target_pairs={{0,17},{1,16},{8,25},{9,24},{16,1},{17,0},{24,9},{25,8},{2,19},{3,... | collective-permute-start | bytes 884744 | tf_op jit(solution)/shard_map/ppermute | solution.py:403
  170.6 46.5 %collective-permute-start.51 = (bf16[72,2048]{1,0:T(8,128)(2,1)}, bf16[72,2048]{1,0:T(8,128)(2,1)}, u32[]{:S(2)}, u32[]{:S(2)}) collective-permute-start(bf16[72,2048]{1,0:T(8,128)(2,1)} %get-tuple-element.154), channel_id=1, source_target_pairs={{0,24},{1,25},{8,16},{9,17},{16,8},{17,9},{24,0},{25,1},{2,26},{3,... | collective-permute-start | bytes 884744 | tf_op jit(solution)/shard_map/ppermute | solution.py:403
  174.6 43.2 %collective-permute-start.52 = (bf16[72,2048]{1,0:T(8,128)(2,1)}, bf16[72,2048]{1,0:T(8,128)(2,1)}, u32[]{:S(2)}, u32[]{:S(2)}) collective-permute-start(bf16[72,2048]{1,0:T(8,128)(2,1)} %get-tuple-element.155), channel_id=1, source_target_pairs={{0,25},{1,24},{8,17},{9,16},{16,9},{17,8},{24,1},{25,0},{2,27},{3,... | collective-permute-start | bytes 884744 | tf_op jit(solution)/shard_map/ppermute | solution.py:403
  197.1 22.5 %collective-permute-start.55 = (bf16[72,2048]{1,0:T(8,128)(2,1)}, bf16[72,2048]{1,0:T(8,128)(2,1)}, u32[]{:S(2)}, u32[]{:S(2)}) collective-permute-start(bf16[72,2048]{1,0:T(8,128)(2,1)} %get-tuple-element.157), channel_id=1, source_target_pairs={{0,1},{1,0},{8,9},{9,8},{16,17},{17,16},{24,25},{25,24},{2,3},{3,2... | collective-permute-start | bytes 884744 | tf_op jit(solution)/shard_map/ppermute | solution.py:403
  198.4 21.4 %collective-permute-start.56 = (bf16[72,2048]{1,0:T(8,128)(2,1)}, bf16[72,2048]{1,0:T(8,128)(2,1)}, u32[]{:S(2)}, u32[]{:S(2)}) collective-permute-start(bf16[72,2048]{1,0:T(8,128)(2,1)} %get-tuple-element.158), channel_id=1, source_target_pairs={{0,8},{1,9},{8,0},{9,1},{16,24},{17,25},{24,16},{25,17},{2,10},{3,... | collective-permute-start | bytes 884744 | tf_op jit(solution)/shard_map/ppermute | solution.py:403
  216.0 22.3 %collective-permute-start.57 = (bf16[72,2048]{1,0:T(8,128)(2,1)}, bf16[72,2048]{1,0:T(8,128)(2,1)S(1)}, u32[]{:S(2)}, u32[]{:S(2)}) collective-permute-start(bf16[72,2048]{1,0:T(8,128)(2,1)} %get-tuple-element.159), channel_id=1, source_target_pairs={{0,9},{1,8},{8,1},{9,0},{16,25},{17,24},{24,17},{25,16},{2,11},{3,... | collective-permute-start | bytes 884744 | tf_op jit(solution)/shard_map/ppermute | solution.py:403
  217.1 22.7 %collective-permute-start.58 = (bf16[72,2048]{1,0:T(8,128)(2,1)}, bf16[72,2048]{1,0:T(8,128)(2,1)S(1)}, u32[]{:S(2)}, u32[]{:S(2)}) collective-permute-start(bf16[72,2048]{1,0:T(8,128)(2,1)} %get-tuple-element.160), channel_id=1, source_target_pairs={{0,16},{1,17},{8,24},{9,25},{16,0},{17,1},{24,8},{25,9},{2,18},{3,... | collective-permute-start | bytes 884744 | tf_op jit(solution)/shard_map/ppermute | solution.py:403
  217.9 22.0 %collective-permute-start.59 = (bf16[72,2048]{1,0:T(8,128)(2,1)}, bf16[72,2048]{1,0:T(8,128)(2,1)S(1)}, u32[]{:S(2)}, u32[]{:S(2)}) collective-permute-start(bf16[72,2048]{1,0:T(8,128)(2,1)} %get-tuple-element.161), channel_id=1, source_target_pairs={{0,17},{1,16},{8,25},{9,24},{16,1},{17,0},{24,9},{25,8},{2,19},{3,... | collective-permute-start | bytes 884744 | tf_op jit(solution)/shard_map/ppermute | solution.py:403
  219.7 24.6 %collective-permute-start.60 = (bf16[72,2048]{1,0:T(8,128)(2,1)}, bf16[72,2048]{1,0:T(8,128)(2,1)S(1)}, u32[]{:S(2)}, u32[]{:S(2)}) collective-permute-start(bf16[72,2048]{1,0:T(8,128)(2,1)} %get-tuple-element.162), channel_id=1, source_target_pairs={{0,24},{1,25},{8,16},{9,17},{16,8},{17,9},{24,0},{25,1},{2,26},{3,... | collective-permute-start | bytes 884744 | tf_op jit(solution)/shard_map/ppermute | solution.py:403
  219.8 25.7 %collective-permute-start.61 = (bf16[72,2048]{1,0:T(8,128)(2,1)}, bf16[72,2048]{1,0:T(8,128)(2,1)S(1)}, u32[]{:S(2)}, u32[]{:S(2)}) collective-permute-start(bf16[72,2048]{1,0:T(8,128)(2,1)} %get-tuple-element.163), channel_id=1, source_target_pairs={{0,25},{1,24},{8,17},{9,16},{16,9},{17,8},{24,1},{25,0},{2,27},{3,... | collective-permute-start | bytes 884744 | tf_op jit(solution)/shard_map/ppermute | solution.py:403
  238.3 40.3 %collective-permute-start.34 = (bf16[72,2048]{1,0:T(8,128)(2,1)}, bf16[72,2048]{1,0:T(8,128)(2,1)S(1)}, u32[]{:S(2)}, u32[]{:S(2)}) collective-permute-start(bf16[72,2048]{1,0:T(8,128)(2,1)} %get-tuple-element.139), channel_id=1, source_target_pairs={{0,1},{1,0},{8,9},{9,8},{16,17},{17,16},{24,25},{25,24},{2,3},{3,2... | collective-permute-start | bytes 884744 | tf_op jit(solution)/shard_map/ppermute | solution.py:403
  239.8 40.1 %collective-permute-start.35 = (bf16[72,2048]{1,0:T(8,128)(2,1)}, bf16[72,2048]{1,0:T(8,128)(2,1)}, u32[]{:S(2)}, u32[]{:S(2)}) collective-permute-start(bf16[72,2048]{1,0:T(8,128)(2,1)} %get-tuple-element.140), channel_id=1, source_target_pairs={{0,8},{1,9},{8,0},{9,1},{16,24},{17,25},{24,16},{25,17},{2,10},{3,... | collective-permute-start | bytes 884744 | tf_op jit(solution)/shard_map/ppermute | solution.py:403
  239.9 41.0 %collective-permute-start.36 = (bf16[72,2048]{1,0:T(8,128)(2,1)}, bf16[72,2048]{1,0:T(8,128)(2,1)}, u32[]{:S(2)}, u32[]{:S(2)}) collective-permute-start(bf16[72,2048]{1,0:T(8,128)(2,1)} %get-tuple-element.141), channel_id=1, source_target_pairs={{0,9},{1,8},{8,1},{9,0},{16,25},{17,24},{24,17},{25,16},{2,11},{3,... | collective-permute-start | bytes 884744 | tf_op jit(solution)/shard_map/ppermute | solution.py:403
  244.3 37.7 %collective-permute-start.37 = (bf16[72,2048]{1,0:T(8,128)(2,1)}, bf16[72,2048]{1,0:T(8,128)(2,1)}, u32[]{:S(2)}, u32[]{:S(2)}) collective-permute-start(bf16[72,2048]{1,0:T(8,128)(2,1)} %get-tuple-element.142), channel_id=1, source_target_pairs={{0,16},{1,17},{8,24},{9,25},{16,0},{17,1},{24,8},{25,9},{2,18},{3,... | collective-permute-start | bytes 884744 | tf_op jit(solution)/shard_map/ppermute | solution.py:403
  245.5 36.7 %collective-permute-start.38 = (bf16[72,2048]{1,0:T(8,128)(2,1)}, bf16[72,2048]{1,0:T(8,128)(2,1)}, u32[]{:S(2)}, u32[]{:S(2)}) collective-permute-start(bf16[72,2048]{1,0:T(8,128)(2,1)} %get-tuple-element.143), channel_id=1, source_target_pairs={{0,17},{1,16},{8,25},{9,24},{16,1},{17,0},{24,9},{25,8},{2,19},{3,... | collective-permute-start | bytes 884744 | tf_op jit(solution)/shard_map/ppermute | solution.py:403
  282.2 19.9 %collective-permute-start.72 = (bf16[72,2048]{1,0:T(8,128)(2,1)}, bf16[72,2048]{1,0:T(8,128)(2,1)S(1)}, u32[]{:S(2)}, u32[]{:S(2)}) collective-permute-start(bf16[72,2048]{1,0:T(8,128)(2,1)} %get-tuple-element.175), channel_id=1, source_target_pairs={{0,9},{1,8},{8,1},{9,0},{16,25},{17,24},{24,17},{25,16},{2,11},{3,... | collective-permute-start | bytes 884744 | tf_op jit(solution)/shard_map/ppermute | solution.py:403
  293.7 22.7 %collective-permute-start.73 = (bf16[72,2048]{1,0:T(8,128)(2,1)}, bf16[72,2048]{1,0:T(8,128)(2,1)S(1)}, u32[]{:S(2)}, u32[]{:S(2)}) collective-permute-start(bf16[72,2048]{1,0:T(8,128)(2,1)} %get-tuple-element.176), channel_id=1, source_target_pairs={{0,16},{1,17},{8,24},{9,25},{16,0},{17,1},{24,8},{25,9},{2,18},{3,... | collective-permute-start | bytes 884744 | tf_op jit(solution)/shard_map/ppermute | solution.py:403
  294.8 22.6 %collective-permute-start.74 = (bf16[72,2048]{1,0:T(8,128)(2,1)}, bf16[72,2048]{1,0:T(8,128)(2,1)S(1)}, u32[]{:S(2)}, u32[]{:S(2)}) collective-permute-start(bf16[72,2048]{1,0:T(8,128)(2,1)} %get-tuple-element.177), channel_id=1, source_target_pairs={{0,17},{1,16},{8,25},{9,24},{16,1},{17,0},{24,9},{25,8},{2,19},{3,... | collective-permute-start | bytes 884744 | tf_op jit(solution)/shard_map/ppermute | solution.py:403
  296.2 26.2 %collective-permute-start.75 = (bf16[72,2048]{1,0:T(8,128)(2,1)}, bf16[72,2048]{1,0:T(8,128)(2,1)S(1)}, u32[]{:S(2)}, u32[]{:S(2)}) collective-permute-start(bf16[72,2048]{1,0:T(8,128)(2,1)} %get-tuple-element.178), channel_id=1, source_target_pairs={{0,24},{1,25},{8,16},{9,17},{16,8},{17,9},{24,0},{25,1},{2,26},{3,... | collective-permute-start | bytes 884744 | tf_op jit(solution)/shard_map/ppermute | solution.py:403
  297.2 26.0 %collective-permute-start.76 = (bf16[72,2048]{1,0:T(8,128)(2,1)}, bf16[72,2048]{1,0:T(8,128)(2,1)S(1)}, u32[]{:S(2)}, u32[]{:S(2)}) collective-permute-start(bf16[72,2048]{1,0:T(8,128)(2,1)} %get-tuple-element.179), channel_id=1, source_target_pairs={{0,25},{1,24},{8,17},{9,16},{16,9},{17,8},{24,1},{25,0},{2,27},{3,... | collective-permute-start | bytes 884744 | tf_op jit(solution)/shard_map/ppermute | solution.py:403
  302.2 26.9 %collective-permute-start.26 = (bf16[72,2048]{1,0:T(8,128)(2,1)S(1)}, bf16[72,2048]{1,0:T(8,128)(2,1)S(1)}, u32[]{:S(2)}, u32[]{:S(2)}) collective-permute-start(bf16[72,2048]{1,0:T(8,128)(2,1)S(1)} %copy-done.38), channel_id=1, source_target_pairs={{0,1},{1,0},{8,9},{9,8},{16,17},{17,16},{24,25},{25,24},{2,3},{3,2... | collective-permute-start | bytes 884744 | tf_op jit(solution)/shard_map/ppermute | solution.py:403
  329.0 26.1 %collective-permute-start.79 = (bf16[128,2048]{1,0:T(8,128)(2,1)}, bf16[128,2048]{1,0:T(8,128)(2,1)S(1)}, u32[]{:S(2)}, u32[]{:S(2)}) collective-permute-start(bf16[128,2048]{1,0:T(8,128)(2,1)} %get-tuple-element.181), channel_id=1, source_target_pairs={{0,2},{2,4},{4,6},{6,0},{1,3},{3,5},{5,7},{7,1},{8,10},{10,12},{12... | collective-permute-start | bytes 1572872 | tf_op jit(solution)/shard_map/ppermute | solution.py:407
  329.7 31.5 %collective-permute-start.77 = (bf16[128,2048]{1,0:T(8,128)(2,1)}, bf16[128,2048]{1,0:T(8,128)(2,1)}, u32[]{:S(2)}, u32[]{:S(2)}) collective-permute-start(bf16[128,2048]{1,0:T(8,128)(2,1)} %get-tuple-element.180), channel_id=1, source_target_pairs={{0,2},{2,4},{4,6},{6,0},{1,3},{3,5},{5,7},{7,1},{8,10},{10,12},{12... | collective-permute-start | bytes 1572872 | tf_op jit(solution)/shard_map/ppermute | solution.py:407
  333.8 19.6 %collective-permute-start.67 = (bf16[72,2048]{1,0:T(8,128)(2,1)}, bf16[72,2048]{1,0:T(8,128)(2,1)S(1)}, u32[]{:S(2)}, u32[]{:S(2)}) collective-permute-start(bf16[72,2048]{1,0:T(8,128)(2,1)} %get-tuple-element.170), channel_id=1, source_target_pairs={{0,24},{1,25},{8,16},{9,17},{16,8},{17,9},{24,0},{25,1},{2,26},{3,... | collective-permute-start | bytes 884744 | tf_op jit(solution)/shard_map/ppermute | solution.py:403
  334.6 19.5 %collective-permute-start.68 = (bf16[72,2048]{1,0:T(8,128)(2,1)}, bf16[72,2048]{1,0:T(8,128)(2,1)S(1)}, u32[]{:S(2)}, u32[]{:S(2)}) collective-permute-start(bf16[72,2048]{1,0:T(8,128)(2,1)} %get-tuple-element.171), channel_id=1, source_target_pairs={{0,25},{1,24},{8,17},{9,16},{16,9},{17,8},{24,1},{25,0},{2,27},{3,... | collective-permute-start | bytes 884744 | tf_op jit(solution)/shard_map/ppermute | solution.py:403
  341.1 27.8 %collective-permute-start.27 = (bf16[72,2048]{1,0:T(8,128)(2,1)}, bf16[72,2048]{1,0:T(8,128)(2,1)}, u32[]{:S(2)}, u32[]{:S(2)}) collective-permute-start(bf16[72,2048]{1,0:T(8,128)(2,1)} %get-tuple-element.132), channel_id=1, source_target_pairs={{0,8},{1,9},{8,0},{9,1},{16,24},{17,25},{24,16},{25,17},{2,10},{3,... | collective-permute-start | bytes 884744 | tf_op jit(solution)/shard_map/ppermute | solution.py:403
  353.4 19.2 %collective-permute-start.28 = (bf16[72,2048]{1,0:T(8,128)(2,1)}, bf16[72,2048]{1,0:T(8,128)(2,1)}, u32[]{:S(2)}, u32[]{:S(2)}) collective-permute-start(bf16[72,2048]{1,0:T(8,128)(2,1)} %get-tuple-element.133), channel_id=1, source_target_pairs={{0,9},{1,8},{8,1},{9,0},{16,25},{17,24},{24,17},{25,16},{2,11},{3,... | collective-permute-start | bytes 884744 | tf_op jit(solution)/shard_map/ppermute | solution.py:403
  354.2 18.6 %collective-permute-start.29 = (bf16[72,2048]{1,0:T(8,128)(2,1)}, bf16[72,2048]{1,0:T(8,128)(2,1)}, u32[]{:S(2)}, u32[]{:S(2)}) collective-permute-start(bf16[72,2048]{1,0:T(8,128)(2,1)} %get-tuple-element.134), channel_id=1, source_target_pairs={{0,16},{1,17},{8,24},{9,25},{16,0},{17,1},{24,8},{25,9},{2,18},{3,... | collective-permute-start | bytes 884744 | tf_op jit(solution)/shard_map/ppermute | solution.py:403
  355.2 19.5 %collective-permute-start.30 = (bf16[72,2048]{1,0:T(8,128)(2,1)}, bf16[72,2048]{1,0:T(8,128)(2,1)}, u32[]{:S(2)}, u32[]{:S(2)}) collective-permute-start(bf16[72,2048]{1,0:T(8,128)(2,1)} %get-tuple-element.135), channel_id=1, source_target_pairs={{0,17},{1,16},{8,25},{9,24},{16,1},{17,0},{24,9},{25,8},{2,19},{3,... | collective-permute-start | bytes 884744 | tf_op jit(solution)/shard_map/ppermute | solution.py:403
  368.8 17.5 %collective-permute-start.41 = (bf16[128,2048]{1,0:T(8,128)(2,1)}, bf16[128,2048]{1,0:T(8,128)(2,1)S(1)}, u32[]{:S(2)}, u32[]{:S(2)}) collective-permute-start(bf16[128,2048]{1,0:T(8,128)(2,1)} %get-tuple-element.146), channel_id=1, source_target_pairs={{0,6},{2,0},{4,2},{6,4},{1,7},{3,1},{5,3},{7,5},{8,14},{10,8},{12,... | collective-permute-start | bytes 1572872 | tf_op jit(solution)/shard_map/ppermute | solution.py:407
  372.6 23.9 %collective-permute-start.42 = (bf16[128,2048]{1,0:T(8,128)(2,1)}, bf16[128,2048]{1,0:T(8,128)(2,1)S(1)}, u32[]{:S(2)}, u32[]{:S(2)}) collective-permute-start(bf16[128,2048]{1,0:T(8,128)(2,1)} %get-tuple-element.147), channel_id=1, source_target_pairs={{0,6},{2,0},{4,2},{6,4},{1,7},{3,1},{5,3},{7,5},{8,14},{10,8},{12,... | collective-permute-start | bytes 1572872 | tf_op jit(solution)/shard_map/ppermute | solution.py:407
  372.7 35.3 %collective-permute-start.80 = (bf16[128,2048]{1,0:T(8,128)(2,1)}, bf16[128,2048]{1,0:T(8,128)(2,1)S(1)}, u32[]{:S(2)}, u32[]{:S(2)}) collective-permute-start(bf16[128,2048]{1,0:T(8,128)(2,1)} %combine.8), channel_id=1, source_target_pairs={{0,2},{2,4},{4,6},{6,0},{1,3},{3,5},{5,7},{7,1},{8,10},{10,12},{12... | collective-permute-start | bytes 1572872 | tf_op jit(solution)/shard_map/ppermute | solution.py:407
  374.7 44.6 %collective-permute-start.78 = (bf16[128,2048]{1,0:T(8,128)(2,1)}, bf16[128,2048]{1,0:T(8,128)(2,1)S(1)}, u32[]{:S(2)}, u32[]{:S(2)}) collective-permute-start(bf16[128,2048]{1,0:T(8,128)(2,1)} %combine.7), channel_id=1, source_target_pairs={{0,2},{2,4},{4,6},{6,0},{1,3},{3,5},{5,7},{7,1},{8,10},{10,12},{12... | collective-permute-start | bytes 1572872 | tf_op jit(solution)/shard_map/ppermute | solution.py:407
  (101 other events, 2527.5 us)
